TPU v7x, 128 devices: a whole 4x4x4 slice. The times are simulated.
128 devices in a mesh: slab: 16 (over z, x), pencil: 8 (over y, core).
Axes of the slice: x: 4, y: 4, z: 4, core: 2. Of those that a mesh axis runs over, the one named last changes fastest.
Arguments:
- a_blocks: float32 [256, 64, 20480], P('slab', 'pencil'), may hold values from -1 to 8, as said below
- col_codes: int32 [256, 64, 5], P('slab', 'pencil'), may hold values from 0 to 8, as said below
- agg_of: int32 [256, 64], P('slab', 'pencil'), may hold values from 0 to 2047, as said below
- test_vectors: float32 [256, 64, 2048], P('slab', 'pencil'), may hold values from -36 to 36
Outputs:
- relaxed: float32 [256, 64, 2048], P('slab', 'pencil')
- tiles: float32 [256, 64, 512], P('slab', 'pencil')
- products: float32 [256, 64, 2560], P('slab', 'pencil')
Inputs may be any that keep to these rules, and one draw needn't show every extreme that they name: `col_codes`: slot 0 of every block row is code 4, the block row itself; slots 1 to 4 hold different codes among the other eight of the 3 x 3 neighbourhood. `agg_of`: aggregate g is owned by device g // 16, devices numbered slab-major. On each device the block rows, in row-major order, form 64 groups of 2 consecutive block rows; all block rows of a group belong to aggregates of one owner, and the groups of one device go to different owners. Some owners receive a group from every device. `a_blocks`: the diagonal entries of every slot-0 block lie in [1.99, 8].
All inputs are finite; a program needn't handle non-finite values.
Results may differ from a plain program's by a relative error of at most 0.0003.
Values sent between devices are 32-bit elements; how exact they have to be, the bound alone decides.
A program may use at most 320 MiB of HBM per device.

v0:
```python
import math

import jax
import jax.numpy as jnp
from jax import lax
from jax.sharding import PartitionSpec as P

BLK = 64
NV = 32
NC = 8
KS = 5
ITERS = 2


OMEGA = 2.0 / 3.0
FULL_PRECISION = lax.Precision.HIGHEST


def with_halo(cells, sides, width):
    for axis, dim in sides:
        count = lax.axis_size(axis)
        ends = count - 1
        head = lax.slice_in_dim(cells, 0, width, axis=dim)
        tail = lax.slice_in_dim(cells, cells.shape[dim] - width, cells.shape[dim], axis=dim)
        cells = jnp.concatenate(
            [
                lax.ppermute(tail, axis, [(i, (i + 1) % count) for i in range(ends)]),
                cells,
                lax.ppermute(head, axis, [((i + 1) % count, i) for i in range(ends)]),
            ],
            axis=dim,
        )
    return cells


def coarse_modes(cells, coarse):
    centre = jnp.arange(cells, dtype=jnp.float32) + 0.5
    order = jnp.arange(coarse, dtype=jnp.float32)
    return jnp.cos(math.pi * centre[:, None] * order[None, :] / cells)


def solve_maps(coarse):
    gram = jnp.einsum("gkv,glv->gkl", coarse, coarse, precision=FULL_PRECISION)
    trace_sum = jnp.trace(gram, axis1=1, axis2=2)
    ridge = 0.1 * trace_sum / NC + 1e-06
    gram = gram + ridge[:, None, None] * jnp.eye(NC, dtype=jnp.float32)[None]
    lower = jnp.linalg.cholesky(gram)
    half_solved = jax.scipy.linalg.solve_triangular(lower, coarse, lower=True)
    solved = jax.scipy.linalg.solve_triangular(lower, half_solved, lower=True, trans=1)
    return jnp.swapaxes(solved, 1, 2)


def slot_index(col_codes):
    height, across_devices = (col_codes.shape[0], col_codes.shape[1])
    row_pos = jnp.arange(height, dtype=jnp.int32)[:, None, None] + col_codes // 3
    col_pos = jnp.arange(across_devices, dtype=jnp.int32)[None, :, None] + col_codes % 3
    return (row_pos * (across_devices + 2) + col_pos).reshape(-1)


def pick_rows(padded, flat_index, height, across_devices):
    features = padded.shape[2]
    flat = padded.reshape(padded.shape[0] * padded.shape[1], features)
    picked = jnp.take(flat, flat_index, axis=0)
    return picked.reshape(height, across_devices, KS, features)


def fit_slots(slot_coefficient, slot_ids, per_owner):
    members = (slot_ids[None, :] == jnp.arange(per_owner, dtype=jnp.int32)[:, None]).astype(
        jnp.float32
    )
    counts = jnp.sum(members, axis=1)
    summed = jnp.dot(
        members,
        slot_coefficient.reshape(slot_coefficient.shape[0], NC * NV),
        precision=FULL_PRECISION,
    )
    coarse = summed.reshape(per_owner, NC, NV) / jnp.maximum(counts, 1.0)[:, None, None]
    maps = solve_maps(coarse)
    return jnp.dot(members.T, maps.reshape(per_owner, NV * NC), precision=FULL_PRECISION)


def pack_slots(chosen_f, payload, group_list, capacity):
    flat = payload.reshape(group_list, capacity * payload.shape[1])
    packed = jnp.dot(chosen_f, flat, precision=FULL_PRECISION)
    return packed.reshape(chosen_f.shape[0], capacity, payload.shape[1])


def unpack_slots(chosen_f, received, block_rows):
    flat = received.reshape(received.shape[0], received.shape[1] * received.shape[2])
    return jnp.dot(chosen_f.T, flat, precision=FULL_PRECISION).reshape(
        block_rows, received.shape[2]
    )


def send_owner(payload, slot_ids):
    arrived, arrived_ids = (
        lax.all_to_all(payload, ("slab", "pencil"), split_axis=0, concat_axis=0, tiled=True),
        lax.all_to_all(slot_ids, ("slab", "pencil"), split_axis=0, concat_axis=0, tiled=True),
    )
    return (arrived, arrived_ids)


def send_back(payload):
    returned = lax.all_to_all(payload, ("slab", "pencil"), split_axis=0, concat_axis=0, tiled=True)
    return returned


def shards(a_blocks, col_codes, agg_of, test_vectors):
    height, across_devices = (agg_of.shape[0], agg_of.shape[1])
    n_slab = lax.axis_size("slab")
    n_pencil = lax.axis_size("pencil")
    devices = n_slab * n_pencil
    blocks = a_blocks.reshape(height, across_devices, KS, BLK, BLK)
    diagonal = jnp.diagonal(blocks[:, :, 0], axis1=-2, axis2=-1)
    block_wide = jnp.transpose(blocks, (0, 1, 3, 2, 4)).reshape(
        height, across_devices, BLK, KS * BLK
    )
    flat_index = slot_index(col_codes)
    candidate_vectors = test_vectors.reshape(height, across_devices, BLK, NV)
    for sweep in range(ITERS):
        padded = with_halo(
            candidate_vectors.reshape(height, across_devices, BLK * NV),
            (("slab", 0), ("pencil", 1)),
            1,
        )
        picked = pick_rows(padded, flat_index, height, across_devices).reshape(
            height, across_devices, KS * BLK, NV
        )
        image = jnp.einsum("ijor,ijrw->ijow", block_wide, picked, precision=FULL_PRECISION)
        candidate_vectors = candidate_vectors - OMEGA * image / diagonal[:, :, :, None]
    squares = jnp.sum(candidate_vectors * candidate_vectors, axis=(0, 1, 2))
    totals = lax.psum(squares, ("slab", "pencil"))
    scale = jnp.sqrt(totals / (height * across_devices * BLK * devices) + 1e-06)
    relaxed = candidate_vectors / scale
    block_rows = height * across_devices
    capacity = 2 * block_rows // devices
    group_list = devices // 2
    per_owner = block_rows // 8
    near_null_modes = coarse_modes(BLK, NC)
    row_vectors = relaxed.reshape(block_rows, BLK, NV)
    group_agg = agg_of.reshape(group_list, capacity)
    group_owner = group_agg[:, 0] // per_owner
    chosen = group_owner[None, :] == jnp.arange(devices, dtype=jnp.int32)[:, None]
    chosen_f = chosen.astype(jnp.float32)
    slot_ids = (
        jnp.sum(jnp.where(chosen[:, :, None], group_agg[None] % per_owner + 1, 0), axis=1) - 1
    )
    slot_count = devices * capacity
    outgoing = pack_slots(chosen_f, row_vectors.reshape(block_rows, BLK * NV), group_list, capacity)
    arrived, arrived_ids = send_owner(outgoing, slot_ids)
    slot_vector_rows = arrived.reshape(slot_count, BLK, NV)
    slot_coefficient = jnp.einsum(
        "wd,xwf->xdf", near_null_modes, slot_vector_rows, precision=FULL_PRECISION
    )
    slot_maps = fit_slots(slot_coefficient, arrived_ids.reshape(slot_count), per_owner)
    slot_tiles = jnp.einsum(
        "scv,svk->sck",
        slot_vector_rows,
        slot_maps.reshape(slot_count, NV, NC),
        precision=FULL_PRECISION,
    )
    returned = send_back(slot_tiles.reshape(devices, capacity, BLK * NC))
    tile_rows = unpack_slots(chosen_f, returned, block_rows).reshape(block_rows, BLK, NC)
    tile_grid = tile_rows.reshape(height, across_devices, BLK * NC)
    padded_tiles = with_halo(tile_grid, (("slab", 0), ("pencil", 1)), 1)
    picked_tiles = pick_rows(padded_tiles, flat_index, height, across_devices).reshape(
        height, across_devices, KS, BLK, NC
    )
    products = jnp.einsum("ijkoc,ijkcw->ijkow", blocks, picked_tiles, precision=FULL_PRECISION)
    return (
        relaxed.reshape(height, across_devices, BLK * NV),
        tile_grid,
        products.reshape(height, across_devices, KS * BLK * NC),
    )


def solution(mesh):
    in_specs = (
        P("slab", "pencil", None),
        P("slab", "pencil", None),
        P("slab", "pencil"),
        P("slab", "pencil", None),
    )
    out_specs = (P("slab", "pencil", None), P("slab", "pencil", None), P("slab", "pencil", None))
    return jax.shard_map(shards, mesh=mesh, in_specs=in_specs, out_specs=out_specs, check_vma=False)
```

profile of v0, /device:TPU:1, one launch (start us, length us, event | category | flops | bytes accessed | tf_op | source)
XLA Modules:
  0.0 638.3 jit_solution(15918062208513373529)
XLA Ops:
  3.0 4.6 collective-permute-start
  10.4 38.9 %copy.177 = f32[16,8,20480]{0,1,2:T(8,128)} copy(f32[16,8,20480]{2,1,0:T(8,128)} %param.6) | data formatting | bytes 20971520 | tf_op args[0]
  49.3 11.6 %slice_bitcast_fusion = f32[16,8,64,64]{0,1,3,2:T(8,128)} fusion(f32[16,8,5,64,64]{0,1,4,3,2:T(8,128)} %bitcast), kind=kLoop, calls=%fused_computation.6 | loop fusion | bytes 4194304 | tf_op jit(solution)/shard_map/squeeze | solution.py:114
  61.7 4.6 collective-permute-start.2
  68.2 2.7 reshape.237
  71.0 3.8 copy.182
  74.7 6.4 %gather_fusion = f32[64,16,8]{1,2,0:T(8,128)S(1)} fusion(f32[16,8,64,64]{0,1,3,2:T(8,128)} %slice_bitcast_fusion, s32[64]{0:T(128)S(1)} %or_bitcast_fusion), kind=kCustom, calls=%fused_computation.2 | custom fusion | bytes 66048 | tf_op jit(solution)/shard_map/jit(diagonal)/gather | solution.py:114
  81.3 63.1 %copy.178 = f32[16,8,64,5,64]{2,4,3,1,0:T(8,128)} copy(f32[16,8,64,5,64]{0,1,4,2,3:T(8,128)} %bitcast.1) | data formatting | bytes 20971520 | tf_op jit(solution)/shard_map/transpose | solution.py:115
  144.8 2.3 copy.176
  148.7 4.6 gather_fusion.2
  153.3 5.2 broadcast_select_fusion.1
  158.5 13.7 %reshape_reshape.7 = f32[16,8,320,32]{3,2,1,0:T(8,128)} reshape(f32[640,2048]{1,0:T(8,128)} %broadcast_select_fusion.1) | data formatting | bytes 10485760 | tf_op jit(solution)/shard_map/reshape;reshape | solution.py:126
  172.2 37.9 %bitcast_subtract_fusion.1 = f32[16,8,64,32]{2,3,1,0:T(8,128)S(1)} fusion(f32[16,8,64,32]{2,3,1,0:T(8,128)} %copy.182, f32[16,8,320,32]{3,2,1,0:T(8,128)} %reshape_reshape.7, f32[16,8,64,320]{2,3,1,0:T(8,128)} %bitcast.82, f32[16,8,64]{2,1,0:T(8,128)S(1)} %copy.181), kind=kOutput, calls=%fused_computation.13 | convolution fusion | flops 1007419392 | bytes 17858560 | tf_op jit(solution)/shard_map/ijor,ijrw->ijow/dot_general | solution.py:129
  210.4 3.1 collective-permute-start.4
  213.6 2.8 copy.184
  218.1 3.6 reshape.242
  222.0 5.0 collective-permute-start.6
  229.7 13.1 %all-to-all-start.1 = ((s32[128,1,2]{2,1,0:T(1,128)}), s32[128,1,2]{2,1,0:T(1,128)S(1)}, u32[]{:S(2)}, u32[]{:S(2)}) async-start(s32[128,1,2]{2,1,0:T(1,128)} %copy.196), calls=%async_computation.1 | async-start | bytes 131072 | tf_op jit(solution)/shard_map/all_to_all | solution.py:98
  246.4 4.6 gather_fusion.3
  251.0 5.2 broadcast_select_fusion
  256.2 13.8 %reshape_reshape.8 = f32[16,8,320,32]{3,2,1,0:T(8,128)} reshape(f32[640,2048]{1,0:T(8,128)} %broadcast_select_fusion) | data formatting | bytes 10485760 | tf_op jit(solution)/shard_map/reshape;reshape | solution.py:126
  270.0 38.3 %multiply_reduce_fusion = (f32[32]{0:T(128)S(1)}, f32[16,8,64,32]{2,3,1,0:T(8,128)}) fusion(f32[16,8,64,32]{2,3,1,0:T(8,128)S(1)} %copy-done.1, f32[16,8,64]{2,1,0:T(8,128)S(1)} %copy.181, f32[16,8,320,32]{3,2,1,0:T(8,128)} %reshape_reshape.8, f32[16,8,64,320]{2,3,1,0:T(8,128)} %bitcast.83), kind=kOutput, calls=%fused_computation.14 | convolution fusion | flops 1007943680 | bytes 17858688 | tf_op jit(solution)/shard_map/ijor,ijrw->ijow/dot_general | solution.py:129
  308.3 67.2 %psum.7 = f32[32]{0:T(128)S(1)} all-reduce(f32[32]{0:T(128)S(1)} %get-tuple-element.33), channel_id=1, replica_groups=mesh['slab'=16,'pencil'=8] {'slab','pencil'}, use_global_device_ids=true, to_apply=%region_1.3 | all-reduce | flops 32 | bytes 256 | tf_op jit(solution)/shard_map/psum | solution.py:132
  375.5 2.0 broadcast_divide_fusion
  377.5 2.8 copy.188
  380.4 3.5 reshape_reshape_reshape.6
  385.0 2.9 copy.192
  388.0 5.2 all-to-all-start
  394.9 28.8 %all-to-all-done = f32[128,2,2048]{2,1,0:T(2,128)S(1)} async-done(((f32[128,2,2048]{2,1,0:T(2,128)}), f32[128,2,2048]{2,1,0:T(2,128)S(1)}, u32[]{:S(2)}, u32[]{:S(2)}) %all-to-all-start) | async-done | bytes 2097184 | tf_op jit(solution)/shard_map/all_to_all | solution.py:97
  423.6 5.3 reshape.246
  429.0 7.0 %copy.197 = f32[256,64,32]{0,1,2:T(8,128)S(1)} copy(f32[256,64,32]{2,1,0:T(8,128)} %reshape.246) | data formatting | bytes 4194304 | tf_op jit(solution)/shard_map/reshape | solution.py:151
  438.2 11.7 %custom-call.11 = f32[16,8,8]{2,1,0:T(8,128)S(1)} custom-call(f32[16,8,8]{2,1,0:T(8,128)S(1)} %fusion.18), custom_call_target="Cholesky" | custom-call | tf_op jit(solution)/shard_map/jit(cholesky)/cholesky | solution.py:47
  450.2 10.0 %custom-call.12 = f32[16,1,8,8]{2,3,1,0:T(8,128)S(1)} custom-call(f32[16,1,8,8]{3,2,1,0:T(8,128)S(1)} %select_bitcast_fusion), custom_call_target="InvertDiagBlocksLowerTriangular" | custom-call | tf_op jit(solution)/shard_map/jit(_solve_triangular)/vmap()/triangular_solve | solution.py:49
  461.6 11.2 %fusion.56 = f32[256,64,8]{2,1,0:T(8,128)} fusion(f32[256,64,32]{2,1,0:T(8,128)} %reshape.246, f32[256,32,8]{1,2,0:T(8,128)S(1)} %copy.209), kind=kOutput, calls=%fused_computation.114 | convolution fusion | flops 50331648 | bytes 2883584 | tf_op jit(solution)/shard_map/scv,svk->sck/dot_general | solution.py:156
  472.8 7.4 %reshape.249 = f32[128,2,512]{2,1,0:T(2,128)} reshape(f32[256,64,8]{2,1,0:T(8,128)} %fusion.56) | data formatting | bytes 1048576 | tf_op jit(solution)/shard_map/reshape | solution.py:162
  480.2 4.3 all-to-all-start.2
  484.7 13.4 %all-to-all-done.2 = f32[128,2,512]{2,1,0:T(2,128)S(1)} async-done(((f32[128,2,512]{2,1,0:T(2,128)}), f32[128,2,512]{2,1,0:T(2,128)S(1)}, u32[]{:S(2)}, u32[]{:S(2)}) %all-to-all-start.2) | async-done | bytes 524320 | tf_op jit(solution)/shard_map/all_to_all | solution.py:104
  498.6 2.2 collective-permute-start.8
  502.3 3.1 collective-permute-done.9
  505.4 3.7 collective-permute-start.10
  509.1 2.1 collective-permute-start.11
  511.3 55.6 %copy.214 = f32[16,8,5,64,64]{4,3,2,1,0:T(8,128)} copy(f32[16,8,5,64,64]{0,1,4,3,2:T(8,128)} %bitcast) | data formatting | bytes 20971520 | tf_op jit(solution)/shard_map/reshape | solution.py:113
  567.0 4.5 reshape.244
  571.7 2.2 gather_fusion.1
  573.8 13.6 %gather.15 = f32[16,8,5,64,8]{4,3,2,1,0:T(8,128)} reshape(f32[640,512]{1,0:T(8,128)S(1)} %gather_fusion.1) | data formatting | bytes 2621440 | tf_op jit(solution)/shard_map/jit(_take)/gather | solution.py:63
  587.4 37.9 %fusion.4 = f32[16,8,5,64,8]{3,4,2,1,0:T(8,128)S(1)} fusion(f32[16,8,5,64,64]{4,3,2,1,0:T(8,128)} %copy.214, f32[16,8,5,64,8]{4,3,2,1,0:T(8,128)} %gather.15, pred[16,8,5]{2,1,0:T(8,128)(4,1)S(1)} %copy.211), kind=kOutput, calls=%fused_computation.16 | convolution fusion | flops 251985920 | bytes 13107840 | tf_op jit(solution)/shard_map/ijkoc,ijkcw->ijkow/dot_general | solution.py:169
  625.3 6.0 copy.215
  631.3 6.8 %copy.216 = f32[16,8,2560]{2,1,0:T(8,128)} copy(f32[16,8,2560]{0,2,1:T(8,128)} %bitcast.84) | data formatting | bytes 2621440
  (112 shorter events, 27.3 us)
Async XLA Ops:
  1.6 60.0 %collective-permute-start.1 = (f32[1,8,2048]{2,0,1:T(1,128)S(1)}, f32[1,8,2048]{2,0,1:T(1,128)S(1)}, u32[]{:S(2)}, u32[]{:S(2)}) collective-permute-start(f32[1,8,2048]{2,0,1:T(1,128)S(1)} %copy.174), channel_id=1, source_target_pairs={{8,0},{16,8},{24,16},{32,24},{40,32},{48,40},{56,48},{64,56},{72,6... | collective-permute-start | bytes 196616 | tf_op jit(solution)/shard_map/ppermute | solution.py:29
  3.0 58.7 %collective-permute-start = (f32[1,8,2048]{2,0,1:T(1,128)S(1)}, f32[1,8,2048]{2,0,1:T(1,128)S(1)}, u32[]{:S(2)}, u32[]{:S(2)}) collective-permute-start(f32[1,8,2048]{2,0,1:T(1,128)S(1)} %copy.173), channel_id=1, source_target_pairs={{0,8},{8,16},{16,24},{24,32},{32,40},{40,48},{48,56},{56,64},{64,7... | collective-permute-start | bytes 196616 | tf_op jit(solution)/shard_map/ppermute | solution.py:27
  10.1 39.3 %copy-start.4 = (s32[16,8,5]{2,1,0:T(8,128)}, s32[16,8,5]{2,1,0:T(8,128)S(1)}, u32[]{:S(2)}) copy-start(s32[16,8,5]{2,1,0:T(8,128)S(1)} %copy.172) | copy-start | bytes 7684
  10.3 39.0 %copy-start.7 = (s32[64]{0:T(128)}, s32[64]{0:T(128)S(1)}, u32[]{:S(2)}) copy-start(s32[64]{0:T(128)S(1)} %and_select_fusion.1) | copy-start | bytes 772
  49.3 11.7 %copy-start.2 = (f32[16,8,2048]{2,1,0:T(8,128)S(1)}, f32[16,8,2048]{2,1,0:T(8,128)}, u32[]{:S(2)}) copy-start(f32[16,8,2048]{2,1,0:T(8,128)} %param.9) | copy-start | bytes 3145732
  61.7 82.7 %collective-permute-start.2 = (f32[18,1,2048]{2,0,1:T(8,128)S(1)}, f32[18,1,2048]{2,0,1:T(8,128)S(1)}, u32[]{:S(2)}, u32[]{:S(2)}) collective-permute-start(f32[18,1,2048]{2,0,1:T(8,128)S(1)} %get-tuple-element.25), channel_id=1, source_target_pairs={{0,1},{1,2},{2,3},{3,4},{4,5},{5,6},{6,7},{8,9},{9,10},{10,11},{11... | collective-permute-start | bytes 442376 | tf_op jit(solution)/shard_map/ppermute | solution.py:27
  66.3 78.2 %collective-permute-start.3 = (f32[18,1,2048]{2,0,1:T(8,128)S(1)}, f32[18,1,2048]{2,0,1:T(8,128)S(1)}, u32[]{:S(2)}, u32[]{:S(2)}) collective-permute-start(f32[18,1,2048]{2,0,1:T(8,128)S(1)} %get-tuple-element.26), channel_id=1, source_target_pairs={{1,0},{2,1},{3,2},{4,3},{5,4},{6,5},{7,6},{9,8},{10,9},{11,10},{12... | collective-permute-start | bytes 442376 | tf_op jit(solution)/shard_map/ppermute | solution.py:29
  210.1 6.4 %copy-start = (f32[16,8,64,32]{2,3,1,0:T(8,128)}, f32[16,8,64,32]{2,3,1,0:T(8,128)S(1)}, u32[]{:S(2)}) copy-start(f32[16,8,64,32]{2,3,1,0:T(8,128)S(1)} %bitcast_subtract_fusion.1) | copy-start | bytes 3145732
  210.4 11.3 %collective-permute-start.4 = (f32[1,8,2048]{2,1,0:T(8,128)S(1)}, f32[1,8,2048]{2,1,0:T(8,128)S(1)}, u32[]{:S(2)}, u32[]{:S(2)}) collective-permute-start(f32[1,8,2048]{2,1,0:T(8,128)S(1)} %slice.78), channel_id=1, source_target_pairs={{0,8},{8,16},{16,24},{24,32},{32,40},{40,48},{48,56},{56,64},{64,7... | collective-permute-start | bytes 196616 | tf_op jit(solution)/shard_map/ppermute | solution.py:27
  216.8 5.1 collective-permute-start.5
  222.0 20.8 %collective-permute-start.6 = (f32[18,1,2048]{2,1,0:T(1,128)S(1)}, f32[18,1,2048]{2,1,0:T(1,128)S(1)}, u32[]{:S(2)}, u32[]{:S(2)}) collective-permute-start(f32[18,1,2048]{2,1,0:T(1,128)S(1)} %get-tuple-element.23), channel_id=1, source_target_pairs={{0,1},{1,2},{2,3},{3,4},{4,5},{5,6},{6,7},{8,9},{9,10},{10,11},{11... | collective-permute-start | bytes 442376 | tf_op jit(solution)/shard_map/ppermute | solution.py:27
  227.0 15.9 %collective-permute-start.7 = (f32[18,1,2048]{2,1,0:T(1,128)S(1)}, f32[18,1,2048]{2,1,0:T(1,128)S(1)}, u32[]{:S(2)}, u32[]{:S(2)}) collective-permute-start(f32[18,1,2048]{2,1,0:T(1,128)S(1)} %get-tuple-element.24), channel_id=1, source_target_pairs={{1,0},{2,1},{3,2},{4,3},{5,4},{6,5},{7,6},{9,8},{10,9},{11,10},{12... | collective-permute-start | bytes 442376 | tf_op jit(solution)/shard_map/ppermute | solution.py:29
  229.7 158.3 %all-to-all-start.1 = ((s32[128,1,2]{2,1,0:T(1,128)}), s32[128,1,2]{2,1,0:T(1,128)S(1)}, u32[]{:S(2)}, u32[]{:S(2)}) async-start(s32[128,1,2]{2,1,0:T(1,128)} %copy.196), calls=%async_computation.1 | async-start | bytes 131072 | tf_op jit(solution)/shard_map/all_to_all | solution.py:98
  256.2 13.8 %copy-start.1 = (f32[16,8,64,32]{2,3,1,0:T(8,128)S(1)}, f32[16,8,64,32]{2,3,1,0:T(8,128)}, u32[]{:S(2)}) copy-start(f32[16,8,64,32]{2,3,1,0:T(8,128)} %copy-done) | copy-start | bytes 3145732
  380.4 3.5 copy-start.8
  388.0 35.6 %all-to-all-start = ((f32[128,2,2048]{2,1,0:T(2,128)}), f32[128,2,2048]{2,1,0:T(2,128)S(1)}, u32[]{:S(2)}, u32[]{:S(2)}) async-start(f32[128,2,2048]{2,1,0:T(2,128)} %copy.192), calls=%async_computation | async-start | bytes 4194304 | tf_op jit(solution)/shard_map/all_to_all | solution.py:97
  472.8 11.7 %copy-start.5 = (s32[16,8,5]{2,1,0:T(8,128)S(1)}, s32[16,8,5]{2,1,0:T(8,128)}, u32[]{:S(2)}) copy-start(s32[16,8,5]{2,1,0:T(8,128)} %copy-done.4) | copy-start | bytes 7684
  480.2 18.0 %all-to-all-start.2 = ((f32[128,2,512]{2,1,0:T(2,128)}), f32[128,2,512]{2,1,0:T(2,128)S(1)}, u32[]{:S(2)}, u32[]{:S(2)}) async-start(f32[128,2,512]{2,1,0:T(2,128)} %reshape.249), calls=%async_computation.2 | async-start | bytes 1048576 | tf_op jit(solution)/shard_map/all_to_all | solution.py:104
  498.6 3.6 collective-permute-start.8
  500.9 66.0 %copy-start.3 = (f32[16,8,512]{2,1,0:T(8,128)}, f32[16,8,512]{2,1,0:T(8,128)S(1)}, u32[]{:S(2)}) copy-start(f32[16,8,512]{2,1,0:T(8,128)S(1)} %reshape_reshape_reshape.7) | copy-start | bytes 786436
  500.9 4.5 collective-permute-start.9
  505.4 66.0 %collective-permute-start.10 = (f32[18,1,512]{2,1,0:T(1,128)S(1)}, f32[18,1,512]{2,1,0:T(1,128)S(1)}, u32[]{:S(2)}, u32[]{:S(2)}) collective-permute-start(f32[18,1,512]{2,1,0:T(1,128)S(1)} %get-tuple-element.29), channel_id=1, source_target_pairs={{0,1},{1,2},{2,3},{3,4},{4,5},{5,6},{6,7},{8,9},{9,10},{10,11},{11... | collective-permute-start | bytes 110600 | tf_op jit(solution)/shard_map/ppermute | solution.py:27
  509.1 62.3 %collective-permute-start.11 = (f32[18,1,512]{2,1,0:T(1,128)S(1)}, f32[18,1,512]{2,1,0:T(1,128)S(1)}, u32[]{:S(2)}, u32[]{:S(2)}) collective-permute-start(f32[18,1,512]{2,1,0:T(1,128)S(1)} %get-tuple-element.30), channel_id=1, source_target_pairs={{1,0},{2,1},{3,2},{4,3},{5,4},{6,5},{7,6},{9,8},{10,9},{11,10},{12... | collective-permute-start | bytes 110600 | tf_op jit(solution)/shard_map/ppermute | solution.py:29
  511.3 55.6 %copy-start.6 = (pred[16,8,5]{0,1,2:T(8,128)(4,1)S(1)}, pred[16,8,5]{0,1,2:T(8,128)(4,1)}, u32[]{:S(2)}) copy-start(pred[16,8,5]{0,1,2:T(8,128)(4,1)} %get-tuple-element.19) | copy-start | bytes 1924
where the time goes:
time: 651 us; the launch traced here: 638 us
  local copies, waits for them, and re-layouts  300 us (46%)
  matrix products  130 us (20%)
  blocking collectives  67.2 us (10%)
  starting transfers between devices  55.6 us (9%)
  waiting for transfers between devices  45.4 us (7%)
  other arithmetic  39.2 us (6%)
    dot_general x2, matrix products, shards(): jnp.einsum('ijor,ijrw->ijow', block_wide, picked, precision=FULL_PRECISION)  76.2 us
    psum x1, blocking collectives, shards(): totals = lax.psum(squares, ('slab', 'pencil'))  67.2 us
    transpose x1, local copies, waits for them, and re-layouts, shards(): jnp.transpose(blocks, (0, 1, 3, 2, 4))  63.1 us
    reshape x1, local copies, waits for them, and re-layouts, shards(): blocks = a_blocks.reshape(height, across_devices, KS, BLK, BLK)  55.6 us
    unnamed x27, local copies, waits for them, and re-layouts  47.3 us
    dot_general x1, matrix products, shards(): jnp.einsum('ijkoc,ijkcw->ijkow', blocks, picked_tiles, precision=FULL_PRE...  37.9 us
    all_to_all x1, waiting for transfers between devices, send_owner(): lax.all_to_all(payload, ('slab', 'pencil'), split_axis=0, concat_axis=0,...  28.8 us
    another operation x2, local copies, waits for them, and re-layouts, shards(): pick_rows(padded, flat_index, height, across_devices)  27.5 us
  transfers between devices with their start and end apart: 15, of which 3 were waited for; matrix products, arithmetic and copies ran while one was open for 44% of the time, Pallas kernels for 0%

commit v1 on v0

v1 whole, which is shorter than its diff:
```python
import math

import numpy as np
import jax
import jax.numpy as jnp
from jax import lax
from jax.experimental import pallas as pl
from jax.experimental.pallas import tpu as pltpu
from jax.sharding import PartitionSpec as P

BLK = 64
NV = 32
NC = 8
KS = 5
OMEGA = 2.0 / 3.0
MESH = pl.DeviceIdType.MESH
F32 = jnp.float32
BF16 = jnp.bfloat16

H = 16
W = 8
PW = W + 2
NB = 4

DIRS = [(1, 0), (-1, 0), (0, 1), (0, -1), (1, 1), (1, -1), (-1, 1), (-1, -1)]


def lanes(shape):
    return lax.broadcasted_iota(jnp.int32, shape, len(shape) - 1)


def lane_group(shape):
    return lanes(shape) // NV


def split2(x):
    hi = x.astype(BF16).astype(F32)
    return hi, x - hi


def split3(x):
    one = x.astype(BF16)
    rest = x - one.astype(F32)
    two = rest.astype(BF16)
    three = (rest - two.astype(F32)).astype(BF16)
    return one, two, three


def by_group(parts, group):
    out = parts[3]
    for n in (2, 1, 0):
        out = jnp.where(group == n, parts[n], out)
    return out


def body(n_slab, n_pencil, a_hbm, codes, agg_s, agg_v, tv, qpat, out_v, out_t, out_p,
         abuf, aprep, dinv, vf, pan0, pan1, tp, vc, tmp, colsend, hrow, hcol, hcor,
         pay, send1, recv1, send2, recv2, xg, xrow, xcol, xcor,
         a_sem, hs_sem, hr_sem, s1, r1, s2, r2):
    devices = n_slab * n_pencil
    slab = lax.axis_index("slab")
    pencil = lax.axis_index("pencil")
    me = slab * n_pencil + pencil

    def a_copy(i):
        return pltpu.make_async_copy(
            a_hbm.at[i], abuf.at[lax.rem(i, NB)], a_sem.at[lax.rem(i, NB)]
        )

    for i in range(NB):
        a_copy(i).start()

    barrier = pltpu.get_barrier_semaphore()

    @pl.loop(1, devices)
    def _(n):
        d = lax.rem(me + n, devices)
        pl.semaphore_signal(
            barrier, inc=1, device_id=(d // n_pencil, lax.rem(d, n_pencil)), device_id_type=MESH
        )

    group16 = lane_group((16, 128))
    group64 = lane_group((64, 128))
    odd64 = lax.rem(group64, 2) == 1

    def spread(x, dst, *lead):
        turns = [x] + [pltpu.roll(x, NV * n, 1) for n in (1, 2, 3)]
        for s in range(4):
            dst[(*lead, pl.ds(s, 16, stride=4), slice(None))] = by_group(
                [turns[(g - s) % 4] for g in range(4)], group16
            )

    def panel_of(v):
        hi, lo = split2(v)
        return jnp.where(odd64, lo, hi).astype(BF16)

    def gather_cells(b):
        return by_group([vf[b, pl.ds(s, 16, stride=4), :] for s in range(4)], group16)

    def edge_copies(rnd, rows):
        copies = []
        for n, (ds, dp) in enumerate(DIRS):
            if dp == 0:
                edge = (H - 1) if ds == 1 else 0
                src = rows.at[edge]
                dst = hrow.at[rnd, n]
            elif ds == 0:
                src = colsend.at[rnd, n - 2]
                dst = hcol.at[rnd, n - 2]
            else:
                edge = (H - 1) if ds == 1 else 0
                src = colsend.at[rnd, 0 if dp == 1 else 1, pl.ds(edge * 16, 16)]
                dst = hcor.at[rnd, n - 4]
            copies.append(remote(src, dst, rnd, n))
        return copies

    def remote(src, dst, rnd, n):
        ds, dp = DIRS[n]
        return pltpu.make_async_remote_copy(
            src_ref=src,
            dst_ref=dst,
            send_sem=hs_sem.at[rnd, n],
            recv_sem=hr_sem.at[rnd, n],
            device_id=(lax.rem(slab + ds + n_slab, n_slab), lax.rem(pencil + dp + n_pencil, n_pencil)),
            device_id_type=MESH,
        )

    def from_inside(n):
        ds, dp = DIRS[n]
        ok_s = slab - ds
        ok_p = pencil - dp
        return jnp.logical_and(
            jnp.logical_and(ok_s >= 0, ok_s < n_slab), jnp.logical_and(ok_p >= 0, ok_p < n_pencil)
        )

    def take_edges(rnd, pan):
        for n, (ds, dp) in enumerate(DIRS):
            keep = from_inside(n).astype(F32)
            if dp == 0:
                base = 0 if ds == 1 else (H + 1) * PW
                for j in range(W):
                    spread(hrow[rnd, n, pl.ds(j, 16, stride=8), :] * keep, tmp, j)
                    pan[base + j + 1] = panel_of(tmp[j])
            elif ds == 0:
                col = 0 if dp == 1 else W + 1

                @pl.loop(0, H // 4)
                def _(q):
                    for u in range(4):
                        i = q * 4 + u
                        start = pl.multiple_of(i * 16, 16)
                        spread(hcol[rnd, n - 2, pl.ds(start, 16), :] * keep, tmp, u)
                        pan[(i + 1) * PW + col] = panel_of(tmp[u])
            else:
                spot = (0 if ds == 1 else H + 1) * PW + (0 if dp == 1 else W + 1)
                spread(hcor[rnd, n - 4] * keep, tmp, n)
                pan[spot] = panel_of(tmp[n])

    for i in range(H):
        colsend[0, 0, i * 16:(i + 1) * 16, :] = tv[i, pl.ds(W - 1, 16, stride=8), :]
        colsend[0, 1, i * 16:(i + 1) * 16, :] = tv[i, pl.ds(0, 16, stride=8), :]
    pl.semaphore_wait(barrier, devices - 1)
    edges0 = edge_copies(0, tv)
    for c in edges0:
        c.start()

    lane32 = lanes((32, 128))
    row32 = lax.broadcasted_iota(jnp.int32, (32, 128), 0)
    left = lane32 < 64

    def eight_rows(even, odd):
        parts = []
        for r in range(4):
            parts += [even[r * 8:(r + 1) * 8], odd[r * 8:(r + 1) * 8]]
        return jnp.concatenate(parts, axis=0)

    @pl.loop(0, H)
    def _(i):
        for j in range(W):
            b = i * W + j
            spread(tv[i, pl.ds(j, 16, stride=8), :], vf, b)
            pan0[(i + 1) * PW + j + 1] = panel_of(vf[b])
        a_copy(i).wait()
        slot = lax.rem(i, NB)
        for j in range(W):
            b = i * W + j
            for k in range(KS):
                x = abuf[slot, pl.ds(k * 256 + j, 32, stride=8), :]
                hi, lo = split2(x)
                even = jnp.where(left, hi, pltpu.roll(lo, 64, 1))
                odd = jnp.where(left, pltpu.roll(hi, 64, 1), lo)
                aprep[b * KS + k] = eight_rows(even, odd).astype(BF16)
                if k == 0:
                    d_even = jnp.sum(jnp.where(lane32 == 2 * row32, x, 0.0), axis=1, keepdims=True)
                    d_odd = jnp.sum(jnp.where(lane32 == 2 * row32 + 65, x, 0.0), axis=1, keepdims=True)
                    dinv[b] = jnp.broadcast_to(OMEGA / eight_rows(d_even, d_odd), (64, 128))

        @pl.when(i + NB < H)
        def _():
            a_copy(i + NB).start()

    for c in edges0:
        c.wait_recv()
    take_edges(0, pan0)

    def slot_spots(i, j):
        b = i * W + j
        spots = []
        for k in range(KS):
            code = codes[b * KS + k]
            di = (code * 11) >> 5
            spots.append((i + di) * PW + j + code - 3 * di)
        return spots

    def relax(i, j, old, new):
        b = i * W + j
        left_side = jnp.concatenate([aprep[b * KS + k] for k in range(KS)], axis=1)
        right = []
        for spot in slot_spots(i, j):
            p = old[spot]
            right += [p, p]
        image = jnp.dot(left_side, jnp.concatenate(right, axis=0), preferred_element_type=F32)
        image = image + pltpu.roll(image, NV, 1)
        step = image * dinv[b]
        for r in range(4):
            for p in range(2):
                tmp[j, pl.ds(r * 16 + p, 8, stride=2), :] = step[(2 * r + p) * 8:(2 * r + p + 1) * 8]
        v = vf[b] - tmp[j]
        vf[b] = v
        new[(i + 1) * PW + j + 1] = panel_of(v)

    def keep_cells(i, j, rnd):
        x = gather_cells(i * W + j)
        vc[i, pl.ds(j, 16, stride=8), :] = x
        if j in (0, W - 1):
            colsend[rnd, 0 if j else 1, pl.ds(pl.multiple_of(i * 16, 16), 16), :] = x

    @pl.loop(0, 2)
    def _(n):
        for j in range(W):
            relax(n * (H - 1), j, pan0, pan1)
        for j in range(W):
            keep_cells(n * (H - 1), j, 1)

    @pl.loop(1, H - 1)
    def _(i):
        for j in (0, W - 1):
            relax(i, j, pan0, pan1)
        for j in (0, W - 1):
            keep_cells(i, j, 1)

    edges1 = edge_copies(1, vc)
    for c in edges1:
        c.start()

    @pl.loop(1, H - 1)
    def _(i):
        for j in range(1, W - 1):
            relax(i, j, pan0, pan1)

    for c in edges1:
        c.wait()
    take_edges(1, pan1)

    @pl.loop(0, H)
    def _(i):
        for j in range(W):
            relax(i, j, pan1, pan0)
        for j in range(W):
            keep_cells(i, j, 2)

    edges2 = edge_copies(2, vc)
    for c in edges2:
        c.start()

    group8 = lane_group((8, 128))

    def coefficients(i, squares):
        sums = [None] * NC
        for q in range(16):
            x = vc[i, q * 8:(q + 1) * 8, :]
            squares = squares + x * x
            for m in range(NC):
                term = x * qpat[m * 16 + q:m * 16 + q + 1, :]
                sums[m] = term if sums[m] is None else sums[m] + term
        folded = []
        for m in range(NC):
            y = sums[m] + pltpu.roll(sums[m], 64, 1)
            folded.append(y + pltpu.roll(y, 32, 1))
        start = pl.multiple_of(i * 8, 8)
        pay[pl.ds(start, 8), 0:128] = by_group(folded[:4], group8)
        pay[pl.ds(start, 8), 128:256] = by_group(folded[4:], group8)
        return squares

    squares = lax.fori_loop(0, H, coefficients, jnp.zeros((8, 128), F32))
    squares = jnp.sum(squares, axis=0, keepdims=True)
    squares = squares + pltpu.roll(squares, 64, 1)
    squares = squares + pltpu.roll(squares, 32, 1)

    lane_d = lanes((devices, 128))
    row_d = lax.broadcasted_iota(jnp.int32, (devices, 128), 0)
    agg = agg_v[...]
    mine = jnp.broadcast_to(agg >> 4, (devices, 128)) == row_d
    local = jnp.broadcast_to((agg & 15) + 1, (devices, 128)).astype(F32)
    parity = lane_d & 1
    parts = jnp.concatenate(split3(pay[...]), axis=0)
    group_d = lane_d // NV
    fifth = jnp.broadcast_to(squares, (devices, 128))
    for cap in range(2):
        chosen = jnp.logical_and(mine, parity == cap).astype(F32)
        chosen_b = chosen.astype(BF16)
        packed = jnp.dot(
            jnp.concatenate([chosen_b] * 3, axis=1), parts, preferred_element_type=F32
        )
        send1[pl.ds(2 * cap, devices, stride=8), :] = packed[:, 0:128]
        send1[pl.ds(2 * cap + 1, devices, stride=8), :] = packed[:, 128:256]
        ident = jnp.sum(chosen * local, axis=1, keepdims=True)
        fifth = jnp.where(group_d == cap + 1, ident, fifth)
    send1[pl.ds(4, devices, stride=8), :] = fifth

    my_rows = pl.ds(pl.multiple_of(me * 8, 8), 8)

    @pl.loop(1, devices)
    def _(n):
        d = lax.rem(me + n, devices)
        pltpu.make_async_remote_copy(
            src_ref=send1.at[pl.ds(pl.multiple_of(d * 8, 8), 8)],
            dst_ref=recv1.at[my_rows],
            send_sem=s1,
            recv_sem=r1,
            device_id=(d // n_pencil, lax.rem(d, n_pencil)),
            device_id_type=MESH,
        ).start()

    own = pltpu.make_async_copy(send1.at[my_rows], recv1.at[my_rows], r1)
    own.start()
    for c in edges2:
        c.wait()
    take_edges(2, pan0)
    pltpu.make_async_copy(send1, recv1, r1).wait()

    heard = recv1[pl.ds(4, devices, stride=8), :]
    total = jnp.sum(heard, axis=0, keepdims=True)
    lane1 = lanes((1, 128))
    total = jnp.where(lane1 < NV, total, 0.0)
    total = total + pltpu.roll(total, 64, 1)
    total = total + pltpu.roll(total, 32, 1)
    inv = 1.0 / jnp.sqrt(total / (H * W * BLK * devices) + 1e-06)

    want = (lane_d + 1).astype(F32)
    few = lane_d < 16
    member_t = [
        jnp.where(jnp.logical_and(pltpu.roll(heard, 128 - NV * (cap + 1), 1) == want, few), 1.0, 0.0)
        for cap in range(2)
    ]
    member = [m.T[0:16] for m in member_t]
    counts = jnp.sum(member[0] + member[1], axis=1, keepdims=True)
    lhs, rhs = [], []
    for cap in range(2):
        rows = jnp.concatenate(
            [recv1[pl.ds(2 * cap + h, devices, stride=8), :] for h in range(2)], axis=1
        )
        lhs += [member[cap].astype(BF16)] * 3
        rhs += list(split3(rows))
    coarse = jnp.dot(
        jnp.concatenate(lhs, axis=1), jnp.concatenate(rhs, axis=0), preferred_element_type=F32
    )
    coarse = coarse * jnp.concatenate([inv, inv], axis=1) / jnp.maximum(counts, 1.0)
    in_first = lanes((16, 128)) < NV
    fit = []
    for k in range(NC):
        half = coarse[:, 128 * (k // 4):128 * (k // 4) + 128]
        if k % 4:
            half = pltpu.roll(half, 128 - NV * (k % 4), 1)
        fit.append(jnp.where(in_first, half, 0.0))
    gram = {}
    for k in range(NC):
        for l in range(k + 1):
            gram[k, l] = jnp.sum(fit[k] * fit[l], axis=1, keepdims=True)
    trace_sum = gram[0, 0]
    for k in range(1, NC):
        trace_sum = trace_sum + gram[k, k]
    ridge = 0.1 * trace_sum / NC + 1e-06
    low, raw, pivot = {}, {}, {}
    for k in range(NC):
        top = gram[k, k] + ridge
        for l in range(k):
            top = top - raw[k, l] * low[k, l]
        pivot[k] = 1.0 / top
        for m in range(k + 1, NC):
            val = gram[m, k]
            for l in range(k):
                val = val - raw[m, l] * low[k, l]
            raw[m, k] = val
            low[m, k] = val * pivot[k]
    sol = []
    for k in range(NC):
        y = fit[k]
        for l in range(k):
            y = y - low[k, l] * sol[l]
        sol.append(y)
    for k in range(NC):
        sol[k] = sol[k] * pivot[k]
    for k in reversed(range(NC)):
        for l in range(k + 1, NC):
            sol[k] = sol[k] - low[l, k] * sol[l]
    columns = []
    for k in range(NC):
        x = sol[k] * inv
        first = x + pltpu.roll(x, 64, 1)
        columns.append(jnp.concatenate([first, pltpu.roll(first, 32, 1)], axis=0))
    table = jnp.concatenate(columns, axis=1)
    pieces = [p for p in split3(table)]
    table = jnp.concatenate(pieces + [jnp.zeros_like(pieces[0])], axis=0)
    pick = member_t[0] + pltpu.roll(member_t[1], 16, 1)
    pick = pick + pltpu.roll(pick, 32, 1) + pltpu.roll(pick, 64, 1)
    replies = jnp.dot(pick.astype(BF16), table, preferred_element_type=F32)
    for k in range(NC):
        send2[pl.ds(k, devices, stride=8), :] = replies[:, 128 * k:128 * (k + 1)]

    @pl.loop(1, devices)
    def _(n):
        d = lax.rem(me + n, devices)
        pltpu.make_async_remote_copy(
            src_ref=send2.at[pl.ds(pl.multiple_of(d * 8, 8), 8)],
            dst_ref=recv2.at[me],
            send_sem=s2,
            recv_sem=r2,
            device_id=(d // n_pencil, lax.rem(d, n_pencil)),
            device_id_type=MESH,
        ).start()

    own = pltpu.make_async_copy(send2.at[my_rows], recv2.at[me], r2)
    own.start()

    @pl.loop(0, H)
    def _(i):
        out_v[i] = vc[i] * inv

    pltpu.make_async_copy(recv2, recv2, r2).wait()

    @pl.loop(0, H)
    def _(i):
        for g in range(W // 2):
            xg[i, g] = recv2[agg_s[i * W + 2 * g] >> 4]

    edges3 = []
    for n, (ds, dp) in enumerate(DIRS):
        if dp == 0:
            edge = (H - 1) if ds == 1 else 0
            edges3.append(remote(xg.at[edge], xrow.at[n], 3, n))
        elif ds == 0:
            edges3.append(remote(xg.at[:, (W // 2 - 1) if dp == 1 else 0], xcol.at[n - 2], 3, n))
        else:
            edge = (H - 1) if ds == 1 else 0
            edges3.append(
                remote(xg.at[edge, (W // 2 - 1) if dp == 1 else 0], xcor.at[n - 4], 3, n)
            )
    for c in edges3:
        c.start()

    even8 = lax.rem(group8, 2) == 0
    high8 = group8 < 2

    def make_tile(spot, x, cap):
        x = jnp.where(even8 if cap == 0 else jnp.logical_not(even8), x, pltpu.roll(x, NV, 1))
        hi, lo = split2(x)
        w = jnp.where(high8, hi, lo)
        w = jnp.concatenate([w] * 16, axis=0).astype(BF16)
        t = lax.dot_general(
            pan0[spot], w, (((1,), (1,)), ((), ())), preferred_element_type=F32
        )
        hi, lo = split2(t)
        tp[spot] = jnp.concatenate([hi, lo], axis=1).astype(BF16)
        return t

    lane8 = lanes((8, 128)) // NC
    sub8 = lax.broadcasted_iota(jnp.int32, (8, 128), 0)
    sub4 = lax.broadcasted_iota(jnp.int32, (4, 128), 0)

    def four_rows(vregs):
        rows = [jnp.sum(v, axis=0, keepdims=True) for v in vregs]
        return jnp.concatenate(rows, axis=0)

    @pl.loop(0, H)
    def _(i):
        for j in range(W):
            t = make_tile((i + 1) * PW + j + 1, xg[i, j // 2], j % 2)
            vregs = [
                jnp.where(
                    lane8 == sub8,
                    t[r * 16:r * 16 + 8],
                    jnp.where(lane8 == sub8 + 8, t[r * 16 + 8:r * 16 + 16], 0.0),
                )
                for r in range(4)
            ]
            out_t[i, pl.ds(j, 4, stride=8), :] = four_rows(vregs)

    for c in edges3:
        c.wait()
    for n, (ds, dp) in enumerate(DIRS):
        if dp == 0:
            base = 0 if ds == 1 else (H + 1) * PW
            for j in range(W):
                make_tile(base + j + 1, xrow[n, j // 2], j % 2)
        elif ds == 0:
            col = 0 if dp == 1 else W + 1

            @pl.loop(0, H // 4)
            def _(q):
                for u in range(4):
                    i = q * 4 + u
                    make_tile((i + 1) * PW + col, xcol[n - 2, i], 1 if dp == 1 else 0)
        else:
            spot = (0 if ds == 1 else H + 1) * PW + (0 if dp == 1 else W + 1)
            make_tile(spot, xcor[n - 4], 1 if dp == 1 else 0)

    @pl.loop(0, H)
    def _(i):
        for j in range(W):
            spots = slot_spots(i, j)
            for k in range(KS):
                t = tp[spots[k]]
                o = jnp.dot(
                    aprep[(i * W + j) * KS + k],
                    jnp.concatenate([t, t], axis=0),
                    preferred_element_type=F32,
                )
                o = o[:, 0:128] + o[:, 128:256]
                vregs = [
                    jnp.where(
                        lane8 == 2 * sub8,
                        o[r * 16:r * 16 + 8],
                        jnp.where(lane8 == 2 * sub8 + 1, o[r * 16 + 8:r * 16 + 16], 0.0),
                    )
                    for r in range(4)
                ]
                out_p[i, pl.ds(k * 32 + j, 4, stride=8), :] = four_rows(vregs)

    for c in edges0:
        c.wait_send()
    others = pl.ds(0, (devices - 1) * 8)
    pltpu.make_async_copy(send1.at[others], recv1.at[others], s1).wait()
    pltpu.make_async_copy(send2.at[others], send2.at[others], s2).wait()


def mode_rows():
    centre = np.arange(BLK, dtype=np.float64) + 0.5
    table = np.cos(math.pi * centre[:, None] * np.arange(NC)[None, :] / BLK)
    rows = table.reshape(16, 4, NC).transpose(2, 0, 1).reshape(NC * 16, 4)
    return np.repeat(rows, NV, axis=1).astype(np.float32)


def solution(mesh):
    n_slab = mesh.shape["slab"]
    n_pencil = mesh.shape["pencil"]
    devices = n_slab * n_pencil

    def shards(a_blocks, col_codes, agg_of, test_vectors):
        a = a_blocks.reshape(H, W, 160, 128).transpose(0, 2, 1, 3).reshape(H, 1280, 128)
        tv = test_vectors.reshape(H, W, 16, 128).transpose(0, 2, 1, 3).reshape(H, 128, 128)
        codes = col_codes.reshape(H * W * KS)
        agg = agg_of.reshape(H * W)
        vmem = pl.BlockSpec(memory_space=pltpu.VMEM)
        smem = pl.BlockSpec(memory_space=pltpu.SMEM)
        out_v, out_t, out_p = pl.pallas_call(
            lambda *refs: body(n_slab, n_pencil, *refs),
            out_shape=(
                jax.ShapeDtypeStruct((H, 128, 128), F32),
                jax.ShapeDtypeStruct((H, 32, 128), F32),
                jax.ShapeDtypeStruct((H, 160, 128), F32),
            ),
            in_specs=[pl.BlockSpec(memory_space=pl.ANY), smem, smem, vmem, vmem, vmem],
            out_specs=(vmem, vmem, vmem),
            scratch_shapes=[
                pltpu.VMEM((NB, 1280, 128), F32),
                pltpu.VMEM((H * W * KS, 64, 128), BF16),
                pltpu.VMEM((H * W, 64, 128), F32),
                pltpu.VMEM((H * W, 64, 128), F32),
                pltpu.VMEM(((H + 2) * PW, 64, 128), BF16),
                pltpu.VMEM(((H + 2) * PW, 64, 128), BF16),
                pltpu.VMEM(((H + 2) * PW, 64, 256), BF16),
                pltpu.VMEM((H, 128, 128), F32),
                pltpu.VMEM((8, 64, 128), F32),
                pltpu.VMEM((3, 2, 256, 128), F32),
                pltpu.VMEM((3, 2, 128, 128), F32),
                pltpu.VMEM((3, 2, 256, 128), F32),
                pltpu.VMEM((3, 4, 16, 128), F32),
                pltpu.VMEM((128, 256), F32),
                pltpu.VMEM((devices * 8, 128), F32),
                pltpu.VMEM((devices * 8, 128), F32),
                pltpu.VMEM((devices * 8, 128), F32),
                pltpu.VMEM((devices, 8, 128), F32),
                pltpu.VMEM((H, W // 2, 8, 128), F32),
                pltpu.VMEM((2, W // 2, 8, 128), F32),
                pltpu.VMEM((2, H, 8, 128), F32),
                pltpu.VMEM((4, 8, 128), F32),
                pltpu.SemaphoreType.DMA((NB,)),
                pltpu.SemaphoreType.DMA((4, 8)),
                pltpu.SemaphoreType.DMA((4, 8)),
                pltpu.SemaphoreType.DMA,
                pltpu.SemaphoreType.DMA,
                pltpu.SemaphoreType.DMA,
                pltpu.SemaphoreType.DMA,
            ],
            compiler_params=pltpu.CompilerParams(
                collective_id=0, has_side_effects=True, vmem_limit_bytes=60 * 1024 * 1024
            ),
        )(a, codes, agg, agg.reshape(1, 128), tv, jnp.asarray(mode_rows()))
        relaxed = out_v.reshape(H, 16, W, 128).transpose(0, 2, 1, 3).reshape(H, W, BLK * NV)
        tiles = out_t.reshape(H, 4, W, 128).transpose(0, 2, 1, 3).reshape(H, W, BLK * NC)
        products = out_p.reshape(H, 20, W, 128).transpose(0, 2, 1, 3).reshape(H, W, KS * BLK * NC)
        return relaxed, tiles, products

    spec = P("slab", "pencil", None)
    return jax.shard_map(
        shards,
        mesh=mesh,
        in_specs=(spec, spec, P("slab", "pencil"), spec),
        out_specs=(spec, spec, spec),
        check_vma=False,
    )
```

time: 651 us -> 98.2 us (0.15); the launches traced: 638 us -> 98 us
  local copies, waits for them, and re-layouts: 300 us -> 7.79 us
  matrix products: 130 us -> 0 us
  Pallas kernels: 0 us -> 89.5 us
  blocking collectives: 67.2 us -> 0 us
  starting transfers between devices: 55.6 us -> 0 us
  waiting for transfers between devices: 45.4 us -> 0 us
  other arithmetic: 39.2 us -> 0 us
    dot_general x10 -> x0, matrix products: 129 us -> none  [the longest x2 76.2 us: shards(): jnp.einsum('ijor,ijrw->ijow', block_wide, picked, precision=FULL_PRECISION)]
    reshape x15 -> x2, local copies, waits for them, and re-layouts: 93.9 us -> 1.39 us  [the longest x1 0.8 us: shards(): codes = col_codes.reshape(H * W * KS)]
    pallas_call x0 -> x1, Pallas kernels: none -> 89.5 us  [shards(): pl.pallas_call(lambda *refs: body(n_slab, n_pencil, *refs), out_shape=(ja...]
    psum x1 -> x0, blocking collectives: 67.2 us -> none  [shards(): totals = lax.psum(squares, ('slab', 'pencil'))]
    transpose x1 -> x0, local copies, waits for them, and re-layouts: 63.1 us -> none  [shards(): jnp.transpose(blocks, (0, 1, 3, 2, 4))]
    all_to_all x3 -> x0, waiting for transfers between devices: 42.2 us -> none  [the longest x1 28.8 us: send_owner(): lax.all_to_all(payload, ('slab', 'pencil'), split_axis=0, concat_axis=0,...]
    unnamed x27 -> x9, local copies, waits for them, and re-layouts: 47.3 us -> 5.79 us
    ppermute x12 -> x0, starting transfers between devices: 32.9 us -> none  [the longest x6 23.1 us: with_halo(): lax.ppermute(tail, axis, [(i, (i + 1) % count) for i in range(ends)])]
  transfers between devices with their start and end apart: 15 -> 0, of which waited for: 3 -> 0; matrix products, arithmetic and copies ran while one was open for 44% -> 0% of each run, Pallas kernels for 0% -> 0%
where the time goes in v1:
time: 98.2 us; the launch traced here: 98 us
  Pallas kernels  89.5 us (91%)
  local copies, waits for them, and re-layouts  7.79 us (8%)
    pallas_call x1, Pallas kernels, shards(): pl.pallas_call(lambda *refs: body(n_slab, n_pencil, *refs), out_shape=(ja...  89.5 us
    unnamed x9, local copies, waits for them, and re-layouts  5.79 us

profile of v1, /device:TPU:1, one launch (start us, length us, event | category | flops | bytes accessed | tf_op | source)
XLA Modules:
  0.0 98.0 jit_solution(14628485284269257208)
XLA Ops:
  0.6 0.8 copy.11
  1.4 0.6 reshape_reshape.3.refs_3_
  2.0 0.6 reshape.45.refs_2_
  2.6 0.9 copy.10
  3.4 0.8 reshape.44.refs_1_
  4.2 89.5 %shard_map.76 = (f32[16,128,128]{2,1,0:T(8,128)}, f32[16,32,128]{2,1,0:T(8,128)}, f32[16,160,128]{2,1,0:T(8,128)}) custom-call(f32[16,1280,128]{2,1,0:T(8,128)} %bitcast.25, s32[640]{0:T(1024)} %reshape.44.refs_1_, s32[128]{0:T(128)} %reshape.45.refs_2_, s32[1,128]{1,0:T(1,128)} %reshape_reshape.3.refs_3_, f32[16,128,128]{2,1,0:T(8,128)} %bitcast.28, ...), custom_call_target="tpu_custom_call" | custom-call | tf_op jit(solution)/shard_map/pallas_call | solution.py:566
  93.8 0.0 copy-start.1
  93.8 0.0 copy-start
  93.8 2.4 %copy.16 = f32[16,8,2048]{2,1,0:T(8,128)} copy(f32[16,8,2048]{2,1,0:T(8,128)} %bitcast.27) | data formatting | bytes 2097152
  96.2 0.0 copy-done.1
  96.2 0.7 copy.17
  96.9 0.0 copy-done
  96.9 1.1 %copy.18 = f32[16,8,2560]{2,1,0:T(8,128)} copy(f32[16,8,2560]{2,1,0:T(8,128)S(1)} %bitcast.26) | data formatting | bytes 2621440
Async XLA Ops:
  93.8 2.4 %copy-start.1 = (f32[16,32,128]{2,1,0:T(8,128)S(1)}, f32[16,32,128]{2,1,0:T(8,128)}, u32[]{:S(2)}) copy-start(f32[16,32,128]{2,1,0:T(8,128)} %get-tuple-element.7) | copy-start | bytes 786436
  93.8 3.1 %copy-start = (f32[16,160,128]{2,1,0:T(8,128)S(1)}, f32[16,160,128]{2,1,0:T(8,128)}, u32[]{:S(2)}) copy-start(f32[16,160,128]{2,1,0:T(8,128)} %get-tuple-element.8) | copy-start | bytes 3932164

commit v2 on v1

v2 whole, which is shorter than its diff:
```python
import math

import ml_dtypes
import numpy as np
import jax
import jax.numpy as jnp
from jax import lax
from jax.experimental import pallas as pl
from jax.experimental.pallas import tpu as pltpu
from jax.sharding import PartitionSpec as P

BLK = 64
NV = 32
NC = 8
KS = 5
OMEGA = 2.0 / 3.0
MESH = pl.DeviceIdType.MESH
F32 = jnp.float32
BF16 = jnp.bfloat16

H = 16
W = 8
PW = W + 2
SPOTS = (H + 2) * PW
NB = 8
SENT1 = 5
SENT2 = 4

DIRS = [(1, 0), (-1, 0), (0, 1), (0, -1), (1, 1), (1, -1), (-1, 1), (-1, -1)]


def lanes(shape):
    return lax.broadcasted_iota(jnp.int32, shape, len(shape) - 1)


def sublanes(shape):
    return lax.broadcasted_iota(jnp.int32, shape, 0)


def lane_group(shape):
    return lanes(shape) // NV


def split2(x):
    hi = x.astype(BF16).astype(F32)
    return hi, x - hi


def split3(x):
    one = x.astype(BF16)
    rest = x - one.astype(F32)
    two = rest.astype(BF16)
    three = (rest - two.astype(F32)).astype(BF16)
    return one, two, three


def by_group(parts, group):
    out = parts[3]
    for n in (2, 1, 0):
        out = jnp.where(group == n, parts[n], out)
    return out


def body(n_slab, n_pencil, a_hbm, codes, agg_s, tv_hbm, modes_hbm, out_v, out_t, out_p,
         abuf, aprep, dinv, vf, pan0, pan1, wbuf, modes, copier, tv, vc, tmp, colsend, hrow, hcol, hcor,
         sq, send1, recv1, send2, recv2, xg, xedge, tiles, prods,
         a_sem, tv_sem, m_sem, o_sem, hs_sem, hr_sem, s1, r1, s2, r2):
    devices = n_slab * n_pencil
    slab = lax.axis_index("slab")
    pencil = lax.axis_index("pencil")
    me = slab * n_pencil + pencil

    def a_copy(i):
        return pltpu.make_async_copy(
            a_hbm.at[i], abuf.at[lax.rem(i, NB)], a_sem.at[lax.rem(i, NB)]
        )

    tv_copy = pltpu.make_async_copy(tv_hbm, tv, tv_sem)
    tv_copy.start()
    for i in range(NB):
        a_copy(i).start()

    m_copy = pltpu.make_async_copy(modes_hbm, modes, m_sem)
    m_copy.start()
    barrier = pltpu.get_barrier_semaphore()

    @pl.loop(1, devices)
    def _(n):
        d = lax.rem(me + n, devices)
        pl.semaphore_signal(
            barrier, inc=1, device_id=(d // n_pencil, lax.rem(d, n_pencil)), device_id_type=MESH
        )

    group16 = lane_group((16, 128))
    group64 = lane_group((64, 128))
    odd64 = lax.rem(group64, 2) == 1
    low64 = group64 < 2
    group32 = lane_group((32, 128))
    odd32 = lax.rem(group32, 2) == 1
    low32 = group32 < 2

    def spread(x, dst, *lead):
        turns = [x] + [pltpu.roll(x, NV * n, 1) for n in (1, 2, 3)]
        for s in range(4):
            dst[(*lead, pl.ds(s, 16, stride=4), slice(None))] = by_group(
                [turns[(g - s) % 4] for g in range(4)], group16
            )

    def panel_of(v):
        hi, lo = split2(v)
        w = jnp.where(odd64, lo, hi)
        both = jnp.concatenate([jnp.where(low64, w, 0.0), jnp.where(low64, 0.0, w)], axis=0)
        return both.astype(BF16)

    def gather_cells(b):
        return by_group([vf[b, pl.ds(s, 16, stride=4), :] for s in range(4)], group16)

    def remote(src, dst, rnd, n):
        ds, dp = DIRS[n]
        return pltpu.make_async_remote_copy(
            src_ref=src,
            dst_ref=dst,
            send_sem=hs_sem.at[rnd, n],
            recv_sem=hr_sem.at[rnd, n],
            device_id=(lax.rem(slab + ds + n_slab, n_slab), lax.rem(pencil + dp + n_pencil, n_pencil)),
            device_id_type=MESH,
        )

    def edge_copies(rnd, rows):
        copies = []
        for n, (ds, dp) in enumerate(DIRS):
            edge = (H - 1) if ds == 1 else 0
            if dp == 0:
                src, dst = rows.at[edge], hrow.at[rnd, n]
            elif ds == 0:
                src, dst = colsend.at[rnd, n - 2], hcol.at[rnd, n - 2]
            else:
                src = colsend.at[rnd, 0 if dp == 1 else 1, pl.ds(edge * 16, 16)]
                dst = hcor.at[rnd, n - 4]
            copies.append(remote(src, dst, rnd, n))
        return copies

    def from_inside(n):
        ds, dp = DIRS[n]
        ok_s = slab - ds
        ok_p = pencil - dp
        return jnp.logical_and(
            jnp.logical_and(ok_s >= 0, ok_s < n_slab), jnp.logical_and(ok_p >= 0, ok_p < n_pencil)
        )

    def take_edges(rnd, pan):
        for n, (ds, dp) in enumerate(DIRS):
            keep = from_inside(n).astype(F32)
            if dp == 0:
                base = 0 if ds == 1 else (H + 1) * PW
                for j in range(W):
                    spread(hrow[rnd, n, pl.ds(j, 16, stride=8), :] * keep, tmp, j)
                    pan[base + j + 1] = panel_of(tmp[j])
            elif ds == 0:
                col = 0 if dp == 1 else W + 1

                @pl.loop(0, H // 8)
                def _(q):
                    for u in range(8):
                        i = q * 8 + u
                        start = pl.multiple_of(i * 16, 16)
                        spread(hcol[rnd, n - 2, pl.ds(start, 16), :] * keep, tmp, u)
                        pan[(i + 1) * PW + col] = panel_of(tmp[u])
            else:
                spot = (0 if ds == 1 else H + 1) * PW + (0 if dp == 1 else W + 1)
                spread(hcor[rnd, n - 4] * keep, tmp, n)
                pan[spot] = panel_of(tmp[n])

    tv_copy.wait()
    for i in range(H):
        colsend[0, 0, i * 16:(i + 1) * 16, :] = tv[i, pl.ds(W - 1, 16, stride=8), :]
        colsend[0, 1, i * 16:(i + 1) * 16, :] = tv[i, pl.ds(0, 16, stride=8), :]

    @pl.loop(0, H)
    def _(i):
        for j in range(W):
            b = i * W + j
            spread(tv[i, pl.ds(j, 16, stride=8), :], vf, b)
            pan0[(i + 1) * PW + j + 1] = panel_of(vf[b])

    lane32 = lanes((32, 128))
    row32 = sublanes((32, 128))
    left = lane32 < 64
    on_even = lane32 == 2 * row32
    on_odd = lane32 == 2 * row32 + 65

    @pl.loop(0, H)
    def _(i):
        a_copy(i).wait()
        slot = lax.rem(i, NB)
        for j in range(W):
            b = i * W + j
            for k in range(KS):
                x = abuf[slot, pl.ds(k * 256 + j, 32, stride=8), :]
                hi = x.astype(BF16)
                lo = (x - hi.astype(F32)).astype(BF16)
                aprep[b * KS + k] = jnp.concatenate([hi, lo], axis=0)
                if k == 0:
                    d_even = jnp.sum(jnp.where(on_even, x, 0.0), axis=1, keepdims=True)
                    d_odd = jnp.sum(jnp.where(on_odd, x, 0.0), axis=1, keepdims=True)
                    dinv[b] = OMEGA / jnp.where(left, d_even, d_odd)

        @pl.when(i + NB < H)
        def _():
            a_copy(i + NB).start()

    lane_r = lanes((128, 128))
    row_r = sublanes((128, 128))
    for n in range(16):
        hit = row_r == n * NC + lax.rem(lane_r, NC)
        copier[:, n * 128:(n + 1) * 128] = jnp.where(hit, 1.0, 0.0).astype(BF16)

    def slot_spots(i, j):
        spots = []
        for k in range(KS):
            code = codes[k, j, i]
            di = (code * 11) >> 5
            spots.append((i + di) * PW + j + code - 3 * di)
        return spots

    def relax(cells, old, new, rnd, kept):
        images = []
        for i, j in cells:
            b = i * W + j
            left_side = jnp.concatenate([aprep[b * KS + k] for k in range(KS)], axis=1)
            right = jnp.concatenate([old[spot] for spot in slot_spots(i, j)], axis=0)
            images.append(jnp.dot(left_side, right, preferred_element_type=F32))
        for n, (i, j) in enumerate(cells):
            r = (images[n][0:32] + images[n][32:64]) * dinv[i * W + j]
            r1, r2, r3 = (pltpu.roll(r, NV * m, 1) for m in (1, 2, 3))
            sums = [r + r3, r + r1, r1 + r2, r2 + r3]
            tmp[n, pl.ds(0, 32, stride=2), :] = by_group(sums, group32)
            tmp[n, pl.ds(1, 32, stride=2), :] = by_group(sums[2:] + sums[:2], group32)
        fresh = [vf[i * W + j] - tmp[n] for n, (i, j) in enumerate(cells)]
        for v, (i, j) in zip(fresh, cells):
            vf[i * W + j] = v
        for v, (i, j) in zip(fresh, cells):
            new[(i + 1) * PW + j + 1] = panel_of(v)
        if kept:
            for n, (i, j) in enumerate(cells):
                keep_cells(i, j, rnd, n)

    def keep_cells(i, j, rnd, n):
        x = gather_cells(i * W + j)
        vc[i, pl.ds(j, 16, stride=8), :] = x
        if j in (0, W - 1):
            colsend[rnd, 0 if j else 1, pl.ds(pl.multiple_of(i * 16, 16), 16), :] = x
        if rnd == 2:
            sq[n] += x * x

    def inside(work, first=1, last=H - 1):
        @pl.loop(0, (last - first) // 2)
        def _(n):
            work([(first + 2 * n + u, j) for u in range(2) for j in range(1, W - 1)])

    def outside(work):
        @pl.loop(0, 2)
        def _(n):
            work([(1 + 7 * n + u, j) for u in range(7) for j in (0, W - 1)])

        @pl.loop(0, 2)
        def _(n):
            work([(n * (H - 1), j) for j in range(W)])

    def first(cells, kept):
        relax(cells, pan0, pan1, 1, kept)

    inside(lambda cells: first(cells, False), 1, 9)
    pl.semaphore_wait(barrier, devices - 1)
    edges0 = edge_copies(0, tv)
    for c in edges0:
        c.start()
    inside(lambda cells: first(cells, False), 9, 15)
    for c in edges0:
        c.wait()
    take_edges(0, pan0)
    outside(lambda cells: first(cells, True))
    edges1 = edge_copies(1, vc)
    for c in edges1:
        c.start()

    sq[...] = jnp.zeros_like(sq)

    def second(cells):
        relax(cells, pan1, pan0, 2, True)

    inside(second)
    for c in edges1:
        c.wait()
    take_edges(1, pan1)
    outside(second)
    edges2 = edge_copies(2, vc)
    for c in edges2:
        c.start()

    squares = sq[0]
    for n in range(1, 16):
        squares = squares + sq[n]
    squares = jnp.sum(squares, axis=0, keepdims=True)
    squares = squares + pltpu.roll(squares, 64, 1)
    squares = squares + pltpu.roll(squares, 32, 1)

    lane_d = lanes((devices, 128))
    row_d = sublanes((devices, 128))
    group_d = lane_d // NV
    lane1 = lanes((1, 128))
    rows = []
    for j in range(W):
        row = jnp.zeros((1, 128), jnp.int32)
        for i in range(H):
            row = jnp.where(lane1 == i * W + j, agg_s[j, i], row)
        rows.append(row)
    while len(rows) > 1:
        rows = [x + y for x, y in zip(rows[::2], rows[1::2])]
    agg = rows[0]
    mine = jnp.broadcast_to(agg >> 4, (devices, 128)) == row_d
    local = jnp.broadcast_to((agg & 15) + 1, (devices, 128)).astype(F32)
    parity = lane_d & 1
    m_copy.wait()
    coef = jnp.zeros((H * W, 2 * 128), F32)
    for q in range(16):
        x = jnp.concatenate([vc[i, q * 8:(q + 1) * 8, :] for i in range(H)], axis=0)
        hi, lo = split2(x)
        coef = coef + jnp.dot(
            jnp.concatenate([hi, lo, hi], axis=1).astype(BF16),
            jnp.concatenate([modes[q, 0:128], modes[q]], axis=0),
            preferred_element_type=F32,
        )
    parts = jnp.concatenate(split3(coef), axis=0)
    fifth = jnp.broadcast_to(squares, (devices, 128))
    for cap in range(2):
        chosen = jnp.logical_and(mine, parity == cap).astype(F32)
        chosen_b = chosen.astype(BF16)
        packed = jnp.dot(
            jnp.concatenate([chosen_b] * 3, axis=1), parts, preferred_element_type=F32
        )
        send1[pl.ds(2 * cap, devices, stride=8), :] = packed[:, 0:128]
        send1[pl.ds(2 * cap + 1, devices, stride=8), :] = packed[:, 128:256]
        ident = jnp.sum(chosen * local, axis=1, keepdims=True)
        fifth = jnp.where(group_d == cap + 1, ident, fifth)
    send1[pl.ds(4, devices, stride=8), :] = fifth

    my_start = pl.multiple_of(me * 8, 8)

    @pl.loop(1, devices)
    def _(n):
        d = lax.rem(me + n, devices)
        pltpu.make_async_remote_copy(
            src_ref=send1.at[pl.ds(pl.multiple_of(d * 8, 8), SENT1)],
            dst_ref=recv1.at[pl.ds(my_start, SENT1)],
            send_sem=s1,
            recv_sem=r1,
            device_id=(d // n_pencil, lax.rem(d, n_pencil)),
            device_id_type=MESH,
        ).start()

    own1 = pltpu.make_async_copy(
        send1.at[pl.ds(my_start, SENT1)], recv1.at[pl.ds(my_start, SENT1)], r1
    )
    own1.start()

    def image_of(cells):
        for i, j in cells:
            b = i * W + j
            spots = slot_spots(i, j)
            for k in range(KS + 1):
                if k < KS:
                    o = jnp.dot(aprep[b * KS + k], pan0[spots[k]], preferred_element_type=F32)
                    r = o[0:32] + o[32:64]
                    z = r + jnp.where(odd32, pltpu.roll(r, NV, 1), pltpu.roll(r, 128 - NV, 1))
                else:
                    z = jnp.where(
                        low32, vf[b, pl.ds(0, 32, stride=2), :], vf[b, pl.ds(1, 32, stride=2), :]
                    )
                hi, lo = split2(z)
                wbuf[b * (KS + 1) + k] = jnp.where(odd32, lo, hi).astype(BF16)

    inside(image_of)

    pltpu.make_async_copy(
        send1.at[pl.ds(0, devices * SENT1)], recv1.at[pl.ds(0, devices * SENT1)], r1
    ).wait()

    heard = recv1[pl.ds(4, devices, stride=8), :]
    total = jnp.sum(heard, axis=0, keepdims=True)
    total = jnp.where(lane1 < NV, total, 0.0)
    total = total + pltpu.roll(total, 64, 1)
    total = total + pltpu.roll(total, 32, 1)
    inv = 1.0 / jnp.sqrt(total / (H * W * BLK * devices) + 1e-06)

    want = (lane_d + 1).astype(F32)
    few = lane_d < 16
    member_t = [
        jnp.where(jnp.logical_and(pltpu.roll(heard, 128 - NV * (cap + 1), 1) == want, few), 1.0, 0.0)
        for cap in range(2)
    ]
    member = [m.T[0:16] for m in member_t]
    counts = jnp.sum(member[0] + member[1], axis=1, keepdims=True)
    lhs, rhs = [], []
    for cap in range(2):
        rows = jnp.concatenate(
            [recv1[pl.ds(2 * cap + h, devices, stride=8), :] for h in range(2)], axis=1
        )
        lhs += [member[cap].astype(BF16)] * 3
        rhs += list(split3(rows))
    coarse = jnp.dot(
        jnp.concatenate(lhs, axis=1), jnp.concatenate(rhs, axis=0), preferred_element_type=F32
    )
    coarse = coarse * jnp.concatenate([inv, inv], axis=1) / jnp.maximum(counts, 1.0)
    in_first = lanes((16, 128)) < NV
    fit = []
    for k in range(NC):
        half = coarse[:, 128 * (k // 4):128 * (k // 4) + 128]
        if k % 4:
            half = pltpu.roll(half, 128 - NV * (k % 4), 1)
        fit.append(jnp.where(in_first, half, 0.0))
    gram = {}
    for k in range(NC):
        for l in range(k + 1):
            gram[k, l] = jnp.sum(fit[k] * fit[l], axis=1, keepdims=True)
    trace_sum = gram[0, 0]
    for k in range(1, NC):
        trace_sum = trace_sum + gram[k, k]
    ridge = 0.1 * trace_sum / NC + 1e-06
    low, raw, pivot = {}, {}, {}
    for k in range(NC):
        top = gram[k, k] + ridge
        for l in range(k):
            top = top - raw[k, l] * low[k, l]
        pivot[k] = 1.0 / top
        for m in range(k + 1, NC):
            val = gram[m, k]
            for l in range(k):
                val = val - raw[m, l] * low[k, l]
            raw[m, k] = val
            low[m, k] = val * pivot[k]
    sol = []
    for k in range(NC):
        y = fit[k]
        for l in range(k):
            y = y - low[k, l] * sol[l]
        sol.append(y)
    for k in range(NC):
        sol[k] = sol[k] * pivot[k]
    for k in reversed(range(NC)):
        for l in range(k + 1, NC):
            sol[k] = sol[k] - low[l, k] * sol[l]
    columns = []
    for r in range(SENT2):
        pair = sol[r] * inv + pltpu.roll(sol[r + 4] * inv, 64, 1)
        columns.append(jnp.concatenate([pair, pltpu.roll(pair, NV, 1)], axis=0))
    pieces = list(split3(jnp.concatenate(columns, axis=1)))
    table = jnp.concatenate(pieces + [jnp.zeros_like(pieces[0])], axis=0)
    pick = member_t[0] + pltpu.roll(member_t[1], 16, 1)
    pick = pick + pltpu.roll(pick, 32, 1) + pltpu.roll(pick, 64, 1)
    replies = jnp.dot(pick.astype(BF16), table, preferred_element_type=F32)
    for r in range(SENT2):
        send2[pl.ds(r, devices, stride=8), :] = replies[:, 128 * r:128 * (r + 1)]

    @pl.loop(1, devices)
    def _(n):
        d = lax.rem(me + n, devices)
        pltpu.make_async_remote_copy(
            src_ref=send2.at[pl.ds(pl.multiple_of(d * 8, 8), SENT2)],
            dst_ref=recv2.at[me, pl.ds(0, SENT2)],
            send_sem=s2,
            recv_sem=r2,
            device_id=(d // n_pencil, lax.rem(d, n_pencil)),
            device_id_type=MESH,
        ).start()

    own2 = pltpu.make_async_copy(
        send2.at[pl.ds(my_start, SENT2)], recv2.at[me, pl.ds(0, SENT2)], r2
    )
    own2.start()

    for c in edges2:
        c.wait()
    take_edges(2, pan0)
    outside(image_of)

    @pl.loop(0, H)
    def _(i):
        vc[i] = vc[i] * inv

    v_copy = pltpu.make_async_copy(vc, out_v, o_sem.at[0])
    v_copy.start()
    pltpu.make_async_copy(
        recv1.at[pl.ds(0, devices * SENT2)], recv1.at[pl.ds(0, devices * SENT2)], r2
    ).wait()

    group8 = lane_group((8, 128))
    low8 = group8 < 2
    sub8 = sublanes((8, 128))

    @pl.loop(0, H)
    def _(i):
        for g in range(W // 2):
            x = recv2[agg_s[2 * g, i] >> 4]
            x = jnp.where(sub8 < 4, x, pltpu.roll(pltpu.roll(x, 4, 0), 64, 1))
            xg[i, g] = x

    edges3 = []
    for n, (ds, dp) in enumerate(DIRS):
        edge = (H - 1) if ds == 1 else 0
        side = (W // 2 - 1) if dp == 1 else 0
        if dp == 0:
            edges3.append(remote(xg.at[edge], xedge.at[pl.ds(4 * n, 4)], 3, n))
        elif ds == 0:
            edges3.append(
                remote(xg.at[:, side], xedge.at[pl.ds(8 + 16 * (n - 2), H)], 3, n)
            )
        else:
            edges3.append(remote(xg.at[edge, side], xedge.at[40 + n - 4], 3, n))
    for c in edges3:
        c.start()

    even_cell = lax.rem(lanes((32, 128)) // NC, 2) == 0
    xw = pan1

    def fit_weights(fits, places):
        t = fits.T[0:64]
        pieces = jnp.concatenate(split2(t), axis=0).astype(BF16)
        for n in range(8):
            o = jnp.dot(pieces, copier[:, n * 256:(n + 1) * 256], preferred_element_type=F32)
            for u in range(2):
                for cap in range(2):
                    place = places[2 * n + u][cap]
                    if place is None:
                        continue
                    parts = []
                    for p in range(2):
                        x = o[64 * p + 32 * cap:64 * p + 32 * cap + 32, 128 * u:128 * u + 128]
                        parts += [jnp.where(even_cell, x, 0.0), jnp.where(even_cell, 0.0, x)]
                    xw[place] = jnp.concatenate(parts, axis=0).astype(BF16)

    @pl.loop(0, 2)
    def _(n):
        for h in range(2):
            i0 = n * 8 + h * 4
            fits = jnp.concatenate([xg[i0 + u, g] for u in range(4) for g in range(W // 2)], axis=0)
            fit_weights(
                fits,
                [
                    [(i0 + u + 1) * PW + 2 * g + cap + 1 for cap in range(2)]
                    for u in range(4)
                    for g in range(W // 2)
                ],
            )

    lane_q = lanes((8, 128)) // 16
    even_s = lax.rem(sub8, 2) == 0
    two_s = lax.rem(sub8 // 2, 2) == 0
    keep1 = lax.rem(lane_q, 2) == lax.rem(sub8, 2)
    at1 = jnp.where(keep1, lane_q, lax.rem(lane_q + 1, 8))
    keep2 = lax.rem(at1 // 2, 2) == lax.rem(sub8 // 2, 2)
    at2 = jnp.where(keep2, at1, lax.rem(at1 + 2, 8))
    keep3 = at2 == sub8

    def own_rows(s):
        z = [s[8 * r:8 * r + 8] for r in range(4)]

        def merge(x, y, first, keep, shift):
            return jnp.where(
                keep, jnp.where(first, x, y), pltpu.roll(jnp.where(first, y, x), shift, 0)
            )

        u = merge(
            merge(z[0], z[1], even_s, keep1, 1), merge(z[2], z[3], even_s, keep1, 1), two_s, keep2, 2
        )
        return jnp.where(keep3, u, pltpu.roll(u, 4, 0))[0:4]

    def finish(cells):
        for i, j in cells:
            b = i * W + j
            spots = slot_spots(i, j) + [(i + 1) * PW + j + 1]
            for k in range(KS + 1):
                w = wbuf[b * (KS + 1) + k]
                x = [xw[spots[k], 32 * m:32 * m + 32] for m in range(4)]
                s = jnp.dot(
                    jnp.concatenate([w, w], axis=1),
                    jnp.concatenate([x[m // 2] for m in range(8)], axis=0),
                    preferred_element_type=F32,
                )
                if k < KS:
                    prods[i, pl.ds(k * 32 + j, 4, stride=8), :] = own_rows(s)
                else:
                    tiles[i, pl.ds(j, 4, stride=8), :] = own_rows(s)

    inside(finish)
    for c in edges3:
        c.wait()
    places = [[None, None] for _ in range(44)]
    for n, (ds, dp) in enumerate(DIRS):
        row = (0 if ds == 1 else H + 1) * PW
        col = 0 if dp == 1 else W + 1
        cap = 1 if dp == 1 else 0
        if dp == 0:
            for j in range(W):
                places[4 * n + j // 2][j % 2] = row + j + 1
        elif ds == 0:
            for i in range(H):
                places[8 + 16 * (n - 2) + i][cap] = (i + 1) * PW + col
        else:
            places[40 + n - 4][cap] = row + col
    for n in range(3):
        tiles16 = [xedge[16 * n + u] for u in range(16 if n < 2 else 12)]
        tiles16 += [jnp.zeros((8, 128), F32)] * (16 - len(tiles16))
        fit_weights(
            jnp.concatenate(tiles16, axis=0), (places + [[None, None]] * 4)[16 * n:16 * n + 16]
        )
    outside(finish)
    t_copy = pltpu.make_async_copy(tiles, out_t, o_sem.at[1])
    p_copy = pltpu.make_async_copy(prods, out_p, o_sem.at[2])
    t_copy.start()
    p_copy.start()

    def sent(rows, sem):
        part = recv1.at[pl.ds(0, (devices - 1) * rows)]
        pltpu.make_async_copy(part, part, sem).wait()

    sent(SENT1, s1)
    sent(SENT2, s2)
    v_copy.wait()
    t_copy.wait()
    p_copy.wait()


def mode_blocks():
    centre = np.arange(BLK, dtype=np.float64) + 0.5
    table = np.cos(math.pi * centre[:, None] * np.arange(NC)[None, :] / BLK).astype(np.float32)
    dense = np.einsum("qsm,vw->qsvmw", table.reshape(16, 4, NC), np.eye(NV, dtype=np.float32))
    dense = dense.reshape(16, 4 * NV, NC * NV)
    hi = dense.astype(ml_dtypes.bfloat16)
    lo = (dense - hi.astype(np.float32)).astype(ml_dtypes.bfloat16)
    return np.concatenate([hi, lo], axis=1)


def solution(mesh):
    n_slab = mesh.shape["slab"]
    n_pencil = mesh.shape["pencil"]
    devices = n_slab * n_pencil

    def shards(a_blocks, col_codes, agg_of, test_vectors):
        a = a_blocks.reshape(H, W, 160, 128).transpose(0, 2, 1, 3).reshape(H, 1280, 128)
        tv = test_vectors.reshape(H, W, 16, 128).transpose(0, 2, 1, 3).reshape(H, 128, 128)
        vmem = pl.BlockSpec(memory_space=pltpu.VMEM)
        smem = pl.BlockSpec(memory_space=pltpu.SMEM)
        hbm = pl.BlockSpec(memory_space=pl.ANY)
        dma = pltpu.SemaphoreType.DMA
        out_v, out_t, out_p = pl.pallas_call(
            lambda *refs: body(n_slab, n_pencil, *refs),
            out_shape=(
                jax.ShapeDtypeStruct((H, 128, 128), F32),
                jax.ShapeDtypeStruct((H, 32, 128), F32),
                jax.ShapeDtypeStruct((H, 160, 128), F32),
            ),
            in_specs=[hbm, smem, smem, hbm, hbm],
            out_specs=(hbm, hbm, hbm),
            scratch_shapes=[
                pltpu.VMEM((NB, 1280, 128), F32),
                pltpu.VMEM((H * W * KS, 64, 128), BF16),
                pltpu.VMEM((H * W, 32, 128), F32),
                pltpu.VMEM((H * W, 64, 128), F32),
                pltpu.VMEM((SPOTS, 128, 128), BF16),
                pltpu.VMEM((SPOTS, 128, 128), BF16),
                pltpu.VMEM((H * W * (KS + 1), 32, 128), BF16),
                pltpu.VMEM((16, 256, 256), BF16),
                pltpu.VMEM((128, 2048), BF16),
                pltpu.VMEM((H, 128, 128), F32),
                pltpu.VMEM((H, 128, 128), F32),
                pltpu.VMEM((16, 64, 128), F32),
                pltpu.VMEM((3, 2, 256, 128), F32),
                pltpu.VMEM((3, 2, 128, 128), F32),
                pltpu.VMEM((3, 2, 256, 128), F32),
                pltpu.VMEM((3, 4, 16, 128), F32),
                pltpu.VMEM((16, 16, 128), F32),
                pltpu.VMEM((devices * 8, 128), F32),
                pltpu.VMEM((devices * 8, 128), F32),
                pltpu.VMEM((devices * 8, 128), F32),
                pltpu.VMEM((devices, 8, 128), F32),
                pltpu.VMEM((H, W // 2, 8, 128), F32),
                pltpu.VMEM((44, 8, 128), F32),
                pltpu.VMEM((H, 32, 128), F32),
                pltpu.VMEM((H, 160, 128), F32),
                dma((NB,)),
                dma,
                dma,
                dma((3,)),
                dma((4, 8)),
                dma((4, 8)),
                dma,
                dma,
                dma,
                dma,
            ],
            compiler_params=pltpu.CompilerParams(
                collective_id=0, has_side_effects=True, vmem_limit_bytes=60 * 1024 * 1024
            ),
        )(a, col_codes.transpose(2, 1, 0), agg_of.T, tv, jnp.asarray(mode_blocks()))
        relaxed = out_v.reshape(H, 16, W, 128).transpose(0, 2, 1, 3).reshape(H, W, BLK * NV)
        tiles = out_t.reshape(H, 4, W, 128).transpose(0, 2, 1, 3).reshape(H, W, BLK * NC)
        products = out_p.reshape(H, 20, W, 128).transpose(0, 2, 1, 3).reshape(H, W, KS * BLK * NC)
        return relaxed, tiles, products

    spec = P("slab", "pencil", None)
    return jax.shard_map(
        shards,
        mesh=mesh,
        in_specs=(spec, spec, P("slab", "pencil"), spec),
        out_specs=(spec, spec, spec),
        check_vma=False,
    )
```

time: 98.2 us -> 72.4 us (0.74)
  Pallas kernels: 89.5 us -> 67.3 us
  local copies, waits for them, and re-layouts: 7.79 us -> 4.18 us
    pallas_call x1, Pallas kernels: 89.5 us -> 67.3 us  [shards(): pl.pallas_call(lambda *refs: body(n_slab, n_pencil, *refs), out_shape=(ja...]
    unnamed x9 -> x7, local copies, waits for them, and re-layouts: 5.79 us -> 4.18 us
    reshape x2 -> x0, local copies, waits for them, and re-layouts: 1.39 us -> none  [the longest x1 0.8 us: shards(): codes = col_codes.reshape(H * W * KS)]
where the time goes in v2:
time: 72.4 us; the launch traced here: 72.1 us
  Pallas kernels  67.3 us (93%)
  local copies, waits for them, and re-layouts  4.18 us (6%)
    pallas_call x1, Pallas kernels, shards(): pl.pallas_call(lambda *refs: body(n_slab, n_pencil, *refs), out_shape=(ja...  67.3 us
    unnamed x7, local copies, waits for them, and re-layouts  4.18 us

profile of v2, /device:TPU:1, one launch (start us, length us, event | category | flops | bytes accessed | tf_op | source)
XLA Modules:
  0.0 72.1 jit_solution(7647032625278560814)
XLA Ops:
  0.6 67.3 %shard_map.76 = (f32[16,128,128]{2,1,0:T(8,128)}, f32[16,32,128]{2,1,0:T(8,128)}, f32[16,160,128]{2,1,0:T(8,128)}) custom-call(f32[16,1280,128]{2,1,0:T(8,128)} %bitcast.27, s32[5,8,16]{2,1,0:T(8,128)} %bitcast.32, s32[8,16]{1,0:T(8,128)} %bitcast.33, f32[16,128,128]{2,1,0:T(8,128)} %bitcast.29, bf16[16,256,256]{2,1,0:T(8,128)(2,1)} %constant.2.clone.refs_4_), custom_call_target="tpu_custom_call" | custom-call | tf_op jit(solution)/shard_map/pallas_call | solution.py:656
  67.9 0.0 copy-start.1
  67.9 0.0 copy-start
  67.9 2.4 %copy.11 = f32[16,8,2048]{2,1,0:T(8,128)} copy(f32[16,8,2048]{2,1,0:T(8,128)} %bitcast.30) | data formatting | bytes 2097152
  70.4 0.0 copy-done.1
  70.4 0.7 copy.12
  71.1 0.0 copy-done
  71.1 1.1 %copy.13 = f32[16,8,2560]{2,1,0:T(8,128)} copy(f32[16,8,2560]{2,1,0:T(8,128)S(1)} %bitcast.28) | data formatting | bytes 2621440
Async XLA Ops:
  67.9 2.4 %copy-start.1 = (f32[16,32,128]{2,1,0:T(8,128)S(1)}, f32[16,32,128]{2,1,0:T(8,128)}, u32[]{:S(2)}) copy-start(f32[16,32,128]{2,1,0:T(8,128)} %get-tuple-element.7) | copy-start | bytes 786436
  67.9 3.1 %copy-start = (f32[16,160,128]{2,1,0:T(8,128)S(1)}, f32[16,160,128]{2,1,0:T(8,128)}, u32[]{:S(2)}) copy-start(f32[16,160,128]{2,1,0:T(8,128)} %get-tuple-element.8) | copy-start | bytes 3932164

commit v3 on v2

--- a/solution.py
+++ b/solution.py
@@ -154,18 +154,16 @@
             if dp == 0:
                 base = 0 if ds == 1 else (H + 1) * PW
                 for j in range(W):
-                    spread(hrow[rnd, n, pl.ds(j, 16, stride=8), :] * keep, tmp, j)
-                    pan[base + j + 1] = panel_of(tmp[j])
+                    spread(hrow[rnd, n, pl.ds(j, 16, stride=8), :] * keep, tmp, n * W + j)
+                for j in range(W):
+                    pan[base + j + 1] = panel_of(tmp[n * W + j])
             elif ds == 0:
                 col = 0 if dp == 1 else W + 1
 
-                @pl.loop(0, H // 8)
-                def _(q):
-                    for u in range(8):
-                        i = q * 8 + u
-                        start = pl.multiple_of(i * 16, 16)
-                        spread(hcol[rnd, n - 2, pl.ds(start, 16), :] * keep, tmp, u)
-                        pan[(i + 1) * PW + col] = panel_of(tmp[u])
+                for i in range(H):
+                    spread(hcol[rnd, n - 2, i * 16:(i + 1) * 16, :] * keep, tmp, i)
+                for i in range(H):
+                    pan[(i + 1) * PW + col] = panel_of(tmp[i])
             else:
                 spot = (0 if ds == 1 else H + 1) * PW + (0 if dp == 1 else W + 1)
                 spread(hcor[rnd, n - 4] * keep, tmp, n)
@@ -263,9 +261,7 @@
         def _(n):
             work([(1 + 7 * n + u, j) for u in range(7) for j in (0, W - 1)])
 
-        @pl.loop(0, 2)
-        def _(n):
-            work([(n * (H - 1), j) for j in range(W)])
+        work([(i, j) for i in (0, H - 1) for j in range(W)])
 
     def first(cells, kept):
         relax(cells, pan0, pan1, 1, kept)
@@ -286,14 +282,14 @@
 
     sq[...] = jnp.zeros_like(sq)
 
-    def second(cells):
+    def again(cells):
         relax(cells, pan1, pan0, 2, True)
 
-    inside(second)
+    inside(again)
     for c in edges1:
         c.wait()
     take_edges(1, pan1)
-    outside(second)
+    outside(again)
     edges2 = edge_copies(2, vc)
     for c in edges2:
         c.start()
@@ -484,9 +480,10 @@
     take_edges(2, pan0)
     outside(image_of)
 
-    @pl.loop(0, H)
-    def _(i):
-        vc[i] = vc[i] * inv
+    @pl.loop(0, 2)
+    def _(n):
+        for u in range(H // 2):
+            vc[n * (H // 2) + u] = vc[n * (H // 2) + u] * inv
 
     v_copy = pltpu.make_async_copy(vc, out_v, o_sem.at[0])
     v_copy.start()
@@ -498,11 +495,12 @@
     low8 = group8 < 2
     sub8 = sublanes((8, 128))
 
-    @pl.loop(0, H)
-    def _(i):
-        for g in range(W // 2):
-            x = recv2[agg_s[2 * g, i] >> 4]
-            x = jnp.where(sub8 < 4, x, pltpu.roll(pltpu.roll(x, 4, 0), 64, 1))
+    @pl.loop(0, 2)
+    def _(n):
+        spots = [(n * (H // 2) + u, g) for u in range(H // 2) for g in range(W // 2)]
+        got = [recv2[agg_s[2 * g, i] >> 4] for i, g in spots]
+        got = [jnp.where(sub8 < 4, x, pltpu.roll(pltpu.roll(x, 4, 0), 64, 1)) for x in got]
+        for (i, g), x in zip(spots, got):
             xg[i, g] = x
 
     edges3 = []
@@ -614,11 +612,22 @@
         fit_weights(
             jnp.concatenate(tiles16, axis=0), (places + [[None, None]] * 4)[16 * n:16 * n + 16]
         )
-    outside(finish)
-    t_copy = pltpu.make_async_copy(tiles, out_t, o_sem.at[1])
-    p_copy = pltpu.make_async_copy(prods, out_p, o_sem.at[2])
-    t_copy.start()
-    p_copy.start()
+    @pl.loop(0, 2)
+    def _(n):
+        finish([(1 + 7 * n + u, j) for u in range(7) for j in (0, W - 1)])
+
+    middle = pl.ds(1, H - 2)
+    t_mid = pltpu.make_async_copy(tiles.at[middle], out_t.at[middle], o_sem.at[1])
+    p_mid = pltpu.make_async_copy(prods.at[middle], out_p.at[middle], o_sem.at[2])
+    t_mid.start()
+    p_mid.start()
+    finish([(i, j) for i in (0, H - 1) for j in range(W)])
+    last = []
+    for n, i in enumerate((0, H - 1)):
+        last.append(pltpu.make_async_copy(tiles.at[i], out_t.at[i], o_sem.at[3 + n]))
+        last.append(pltpu.make_async_copy(prods.at[i], out_p.at[i], o_sem.at[5 + n]))
+    for c in last:
+        c.start()
 
     def sent(rows, sem):
         part = recv1.at[pl.ds(0, (devices - 1) * rows)]
@@ -626,9 +635,8 @@
 
     sent(SENT1, s1)
     sent(SENT2, s2)
-    v_copy.wait()
-    t_copy.wait()
-    p_copy.wait()
+    for c in [v_copy, t_mid, p_mid] + last:
+        c.wait()
 
 
 def mode_blocks():
@@ -691,7 +699,7 @@
                 dma((NB,)),
                 dma,
                 dma,
-                dma((3,)),
+                dma((7,)),
                 dma((4, 8)),
                 dma((4, 8)),
                 dma,

time: 72.4 us -> 69.2 us (0.956)
  Pallas kernels: 67.3 us -> 64.2 us
    pallas_call x1, Pallas kernels: 67.3 us -> 64.2 us  [shards(): pl.pallas_call(lambda *refs: body(n_slab, n_pencil, *refs), out_shape=(ja...]
where the time goes in v3:
time: 69.2 us; the launch traced here: 69 us
  Pallas kernels  64.2 us (93%)
  local copies, waits for them, and re-layouts  4.18 us (6%)
    pallas_call x1, Pallas kernels, shards(): pl.pallas_call(lambda *refs: body(n_slab, n_pencil, *refs), out_shape=(ja...  64.2 us
    unnamed x7, local copies, waits for them, and re-layouts  4.18 us

profile of v3, /device:TPU:1, one launch (start us, length us, event | category | flops | bytes accessed | tf_op | source)
XLA Modules:
  0.0 69.0 jit_solution(12376440050607786167)
XLA Ops:
  0.6 64.2 %shard_map.76 = (f32[16,128,128]{2,1,0:T(8,128)}, f32[16,32,128]{2,1,0:T(8,128)}, f32[16,160,128]{2,1,0:T(8,128)}) custom-call(f32[16,1280,128]{2,1,0:T(8,128)} %bitcast.27, s32[5,8,16]{2,1,0:T(8,128)} %bitcast.32, s32[8,16]{1,0:T(8,128)} %bitcast.33, f32[16,128,128]{2,1,0:T(8,128)} %bitcast.29, bf16[16,256,256]{2,1,0:T(8,128)(2,1)} %constant.2.clone.refs_4_), custom_call_target="tpu_custom_call" | custom-call | tf_op jit(solution)/shard_map/pallas_call | solution.py:664
  64.8 0.0 copy-start.1
  64.8 0.0 copy-start
  64.8 2.4 %copy.11 = f32[16,8,2048]{2,1,0:T(8,128)} copy(f32[16,8,2048]{2,1,0:T(8,128)} %bitcast.30) | data formatting | bytes 2097152
  67.2 0.0 copy-done.1
  67.2 0.7 %copy.12 = f32[16,8,512]{2,1,0:T(8,128)} copy(f32[16,8,512]{2,1,0:T(8,128)S(1)} %bitcast.31) | data formatting | bytes 524288
  68.0 0.0 copy-done
  68.0 1.1 %copy.13 = f32[16,8,2560]{2,1,0:T(8,128)} copy(f32[16,8,2560]{2,1,0:T(8,128)S(1)} %bitcast.28) | data formatting | bytes 2621440
Async XLA Ops:
  64.8 2.4 %copy-start.1 = (f32[16,32,128]{2,1,0:T(8,128)S(1)}, f32[16,32,128]{2,1,0:T(8,128)}, u32[]{:S(2)}) copy-start(f32[16,32,128]{2,1,0:T(8,128)} %get-tuple-element.7) | copy-start | bytes 786436
  64.8 3.1 %copy-start = (f32[16,160,128]{2,1,0:T(8,128)S(1)}, f32[16,160,128]{2,1,0:T(8,128)}, u32[]{:S(2)}) copy-start(f32[16,160,128]{2,1,0:T(8,128)} %get-tuple-element.8) | copy-start | bytes 3932164

commit v4 on v3

--- a/solution.py
+++ b/solution.py
@@ -174,12 +174,13 @@
         colsend[0, 0, i * 16:(i + 1) * 16, :] = tv[i, pl.ds(W - 1, 16, stride=8), :]
         colsend[0, 1, i * 16:(i + 1) * 16, :] = tv[i, pl.ds(0, 16, stride=8), :]
 
-    @pl.loop(0, H)
-    def _(i):
-        for j in range(W):
-            b = i * W + j
-            spread(tv[i, pl.ds(j, 16, stride=8), :], vf, b)
-            pan0[(i + 1) * PW + j + 1] = panel_of(vf[b])
+    @pl.loop(0, H // 2)
+    def _(n):
+        cells = [(2 * n + u, j) for u in range(2) for j in range(W)]
+        for i, j in cells:
+            spread(tv[i, pl.ds(j, 16, stride=8), :], vf, i * W + j)
+        for i, j in cells:
+            pan0[(i + 1) * PW + j + 1] = panel_of(vf[i * W + j])
 
     lane32 = lanes((32, 128))
     row32 = sublanes((32, 128))
@@ -251,10 +252,10 @@
         if rnd == 2:
             sq[n] += x * x
 
-    def inside(work, first=1, last=H - 1):
-        @pl.loop(0, (last - first) // 2)
+    def inside(work, first=1, last=H - 1, rows=2):
+        @pl.loop(0, (last - first) // rows)
         def _(n):
-            work([(first + 2 * n + u, j) for u in range(2) for j in range(1, W - 1)])
+            work([(first + rows * n + u, j) for u in range(rows) for j in range(1, W - 1)])
 
     def outside(work):
         @pl.loop(0, 2)
@@ -266,12 +267,12 @@
     def first(cells, kept):
         relax(cells, pan0, pan1, 1, kept)
 
-    inside(lambda cells: first(cells, False), 1, 9)
+    inside(lambda cells: first(cells, False), 1, 9, 4)
     pl.semaphore_wait(barrier, devices - 1)
     edges0 = edge_copies(0, tv)
     for c in edges0:
         c.start()
-    inside(lambda cells: first(cells, False), 9, 15)
+    inside(lambda cells: first(cells, False), 9, 15, 3)
     for c in edges0:
         c.wait()
     take_edges(0, pan0)
@@ -285,7 +286,8 @@
     def again(cells):
         relax(cells, pan1, pan0, 2, True)
 
-    inside(again)
+    inside(again, 1, 9, 4)
+    inside(again, 9, 15, 3)
     for c in edges1:
         c.wait()
     take_edges(1, pan1)
@@ -295,7 +297,7 @@
         c.start()
 
     squares = sq[0]
-    for n in range(1, 16):
+    for n in range(1, 24):
         squares = squares + sq[n]
     squares = jnp.sum(squares, axis=0, keepdims=True)
     squares = squares + pltpu.roll(squares, 64, 1)
@@ -682,12 +684,12 @@
                 pltpu.VMEM((128, 2048), BF16),
                 pltpu.VMEM((H, 128, 128), F32),
                 pltpu.VMEM((H, 128, 128), F32),
-                pltpu.VMEM((16, 64, 128), F32),
+                pltpu.VMEM((24, 64, 128), F32),
                 pltpu.VMEM((3, 2, 256, 128), F32),
                 pltpu.VMEM((3, 2, 128, 128), F32),
                 pltpu.VMEM((3, 2, 256, 128), F32),
                 pltpu.VMEM((3, 4, 16, 128), F32),
-                pltpu.VMEM((16, 16, 128), F32),
+                pltpu.VMEM((24, 16, 128), F32),
                 pltpu.VMEM((devices * 8, 128), F32),
                 pltpu.VMEM((devices * 8, 128), F32),
                 pltpu.VMEM((devices * 8, 128), F32),

time: 69.2 us -> 67.8 us (0.980)
  Pallas kernels: 64.2 us -> 62.7 us
    pallas_call x1, Pallas kernels: 64.2 us -> 62.7 us  [shards(): pl.pallas_call(lambda *refs: body(n_slab, n_pencil, *refs), out_shape=(ja...]
where the time goes in v4:
time: 67.8 us; the launch traced here: 67.5 us
  Pallas kernels  62.7 us (92%)
  local copies, waits for them, and re-layouts  4.18 us (6%)
    pallas_call x1, Pallas kernels, shards(): pl.pallas_call(lambda *refs: body(n_slab, n_pencil, *refs), out_shape=(ja...  62.7 us
    unnamed x7, local copies, waits for them, and re-layouts  4.18 us

profile of v4, /device:TPU:1, one launch (start us, length us, event | category | flops | bytes accessed | tf_op | source)
XLA Modules:
  0.0 67.5 jit_solution(16762513552309069970)
XLA Ops:
  0.6 62.7 %shard_map.76 = (f32[16,128,128]{2,1,0:T(8,128)}, f32[16,32,128]{2,1,0:T(8,128)}, f32[16,160,128]{2,1,0:T(8,128)}) custom-call(f32[16,1280,128]{2,1,0:T(8,128)} %bitcast.27, s32[5,8,16]{2,1,0:T(8,128)} %bitcast.32, s32[8,16]{1,0:T(8,128)} %bitcast.33, f32[16,128,128]{2,1,0:T(8,128)} %bitcast.29, bf16[16,256,256]{2,1,0:T(8,128)(2,1)} %constant.2.clone.refs_4_), custom_call_target="tpu_custom_call" | custom-call | tf_op jit(solution)/shard_map/pallas_call | solution.py:666
  63.3 0.0 copy-start.1
  63.3 0.0 copy-start
  63.4 2.4 %copy.11 = f32[16,8,2048]{2,1,0:T(8,128)} copy(f32[16,8,2048]{2,1,0:T(8,128)} %bitcast.30) | data formatting | bytes 2097152
  65.8 0.0 copy-done.1
  65.8 0.7 %copy.12 = f32[16,8,512]{2,1,0:T(8,128)} copy(f32[16,8,512]{2,1,0:T(8,128)S(1)} %bitcast.31) | data formatting | bytes 524288
  66.5 0.0 copy-done
  66.5 1.1 %copy.13 = f32[16,8,2560]{2,1,0:T(8,128)} copy(f32[16,8,2560]{2,1,0:T(8,128)S(1)} %bitcast.28) | data formatting | bytes 2621440
Async XLA Ops:
  63.3 2.4 %copy-start.1 = (f32[16,32,128]{2,1,0:T(8,128)S(1)}, f32[16,32,128]{2,1,0:T(8,128)}, u32[]{:S(2)}) copy-start(f32[16,32,128]{2,1,0:T(8,128)} %get-tuple-element.7) | copy-start | bytes 786436
  63.3 3.1 %copy-start = (f32[16,160,128]{2,1,0:T(8,128)S(1)}, f32[16,160,128]{2,1,0:T(8,128)}, u32[]{:S(2)}) copy-start(f32[16,160,128]{2,1,0:T(8,128)} %get-tuple-element.8) | copy-start | bytes 3932164
